TPU v7x, 32 devices: a whole 2x2x4 slice. The times are simulated.
32 devices in a mesh: groups: 2 (over x), ctx: 16 (over z, y, core).
Axes of the slice: x: 2, y: 2, z: 4, core: 2. Of those that a mesh axis runs over, the one named last changes fastest.
Arguments:
- query_rows: float32 [8192, 768], P(('groups', 'ctx')), parts along dimension 0, may hold values from -6 to 6
- key_rows: float32 [8192, 768], P(('groups', 'ctx')), parts along dimension 0, may hold values from -6 to 6
- value_rows: float32 [8192, 768], P(('groups', 'ctx')), parts along dimension 0, may hold values from -6 to 6
- grad_rows: float32 [8192, 768], P(('groups', 'ctx')), parts along dimension 0, may hold values from -6 to 6
- placement: int32 [128], P(('groups', 'ctx')), parts along dimension 0, may hold values from 0 to 63, as said below
- cell_lengths: int32 [128], P(('groups', 'ctx')), parts along dimension 0, may hold values from 16 to 64
- gene_mask: int32 [128, 3], P(('groups', 'ctx')), parts along dimension 0, may hold values 0 or 1
Outputs:
- grad_queries: float32 [8192, 768], P(('groups', 'ctx')), parts along dimension 0
- grad_keys: float32 [8192, 768], P(('groups', 'ctx')), parts along dimension 0
- grad_values: float32 [8192, 768], P(('groups', 'ctx')), parts along dimension 0
There are 2 independent parts, one for each index of `groups`. A program takes and returns all parts, laid end to end along the dimension named above; each array names one. Nothing has to cross between parts.
Inputs may be any that keep to these rules, and one draw needn't show every extreme that they name: `placement`: A permutation of the slots. The cells of ctx index d (cells d * 4 to d * 4 + 3) take slots of block d or of block (d + 1) mod 16; exactly 2 of them take slots of the next block.
All inputs are finite; a program needn't handle non-finite values. No bound on the sum of `gene_mask` on one device may be relied on, other than what follows from the above.
Results may differ from a plain program's by a relative error of at most 0.0003.
Values sent between devices are 32-bit elements; how exact they have to be, the bound alone decides.
No kernel may reach another device: no remote copies, remote signals or barrier semaphores. Data moves between devices by JAX's collectives and lax.ppermute only.
A program may use at most 64 MiB of HBM per device.

v0:
```python
import functools

import jax
import jax.numpy as jnp
from jax import lax
from jax.experimental import pallas as pl
from jax.experimental.pallas import tpu as pltpu
from jax.sharding import PartitionSpec as P

HEAD_DIM = 64
CELL = 64
CELLS = 4
ROWS = 256
PLANE = 4
HEADS = 3
HALO = 14
F32 = jnp.float32
BF16 = jnp.bfloat16
VMEM = pltpu.VMEM
NEGATIVE = -1e30
SCALE = HEAD_DIM ** -0.5


def vspec():
    return pl.BlockSpec(memory_space=pltpu.VMEM)


def sspec():
    return pl.BlockSpec(memory_space=pltpu.SMEM)


def params(limit=32):
    return pltpu.CompilerParams(vmem_limit_bytes=limit << 20)


def cost(flops, nbytes):
    return pl.CostEstimate(flops=flops, bytes_accessed=nbytes, transcendentals=0)


def lanes(shape):
    return lax.broadcasted_iota(jnp.int32, shape, 1)


def swap_half(x):
    return pltpu.roll(x, 64, 1)


def join(low, high):
    return jnp.where(lanes(low.shape) < 64, low, high)


def cells(i):
    return pl.ds(pl.multiple_of(i * CELL, CELL), CELL)


def pack_kernel(first_of, with_meta, info, a_hbm, b_hbm, *refs):
    mine, core, ys = refs[0], refs[1], refs[2:8]
    a_ref, b_ref, sems = refs[8:]
    copies = []
    for i, (src, dst) in enumerate(((a_hbm, a_ref), (b_hbm, b_ref))):
        for c in range(CELLS):
            r = pl.ds(c * CELL, CELL)
            copies.append(pltpu.make_async_copy(src.at[r], dst.at[r], sems.at[i, c]))
            copies[-1].start()
    me = info[24]
    if with_meta:
        lane = lax.broadcasted_iota(jnp.int32, (8, 128), 1)
        meta = jnp.zeros((8, 128), F32)
        for i in range(20):
            meta = jnp.where(lane == i, info[i].astype(F32), meta)
        mine[pl.ds(HEADS * ROWS, 8), :] = meta
        core[pl.ds(HEADS * ROWS, 8), :] = meta
        ys[0][pl.ds(ROWS, 8), :] = meta
        ys[1][pl.ds(ROWS, 8), :] = meta
    row = lax.broadcasted_iota(jnp.int32, (CELL, 128), 0)
    for c in range(CELLS):
        copies[c].wait()
        copies[CELLS + c].wait()
        r = pl.ds(c * CELL, CELL)
        for s in range(PLANE):
            j = lax.bitwise_xor(me, s)
            first = pl.ds(pl.multiple_of(j * 128, 128), 128)
            last = pl.ds(pl.multiple_of((4 + j // 2) * 128, 128), 128)
            odd = (j % 2) == 1
            a, b = first_of(info, row, c, a_ref[r, first], b_ref[r, first])
            x, y = first_of(info, row, c, a_ref[r, last], b_ref[r, last])
            x = jnp.where(odd, swap_half(x), x)
            y = jnp.where(odd, y, swap_half(y))
            heads = (join(a, swap_half(b)), join(swap_half(a), b), join(x, y))
            for h in range(HEADS):
                if s == 0:
                    mine[pl.ds(h * ROWS + c * CELL, CELL), :] = heads[h]
                elif s == 1:
                    core[pl.ds(h * ROWS + c * CELL, CELL), :] = heads[h]
                else:
                    ys[2 * h + s - 2][pl.ds(c * CELL, CELL), :] = heads[h]


def plain(info, row, c, a, b):
    return a, b


def scaled(info, row, c, a, b):
    return a * SCALE, jnp.where(row < info[4 + c], b, 0.0)


def pack_heads(first_of, with_meta, info, a, b):
    extra = 8 if with_meta else 0
    shapes = [(HEADS * ROWS + extra, 128)] * 2 + [(ROWS + extra, 128)] * 2 + [(ROWS, 128)] * 4
    return pl.pallas_call(
        functools.partial(pack_kernel, first_of, with_meta),
        out_shape=[jax.ShapeDtypeStruct(s, F32) for s in shapes],
        in_specs=[sspec()] + [pl.BlockSpec(memory_space=pltpu.HBM)] * 2,
        out_specs=[vspec()] * 8,
        scratch_shapes=[
            VMEM(a.shape, F32),
            VMEM(b.shape, F32),
            pltpu.SemaphoreType.DMA((2, CELLS)),
        ],
        compiler_params=params(),
        cost_estimate=cost(1 << 20, 3 << 20),
        name="pack_heads",
    )(info, a, b)


def walk(meta, start, total, visit):
    rank = jnp.int32(0)
    for s in range(PLANE):
        for c in range(CELLS):
            rel = lax.rem(meta[s, c] - start + total, total)
            moved = rel >= 16
            slot = jnp.where(moved, 12 + rank, rel - 4)
            visit(s, c, rel, slot)
            rank = rank + moved.astype(jnp.int32)


def row_of(h):
    return (h * ROWS, h * ROWS, 0, 0)


META_ROWS = (HEADS * ROWS, HEADS * ROWS, ROWS, ROWS)


def halo_kernel(total, h, info, meta, *refs):
    kv, out = refs[:4], refs[4]

    def visit(s, c, rel, slot):
        @pl.when(rel >= 4)
        def _():
            out[cells(slot), :] = kv[s][pl.ds(row_of(h)[s] + c * CELL, CELL), :]

    walk(meta, info[25], total, visit)
    if h == 0:
        out[pl.ds(HALO * CELL, 8), :] = jnp.zeros((8, 128), F32)
        for s in range(PLANE):
            out[pl.ds(HALO * CELL + s, 1), :] = kv[s][pl.ds(META_ROWS[s], 1), :]


def halo_message(total, h, info, meta, kv):
    rows = HALO * CELL + (8 if h == 0 else 0)
    return pl.pallas_call(
        functools.partial(halo_kernel, total, h),
        out_shape=jax.ShapeDtypeStruct((rows, 128), F32),
        in_specs=[sspec()] * 2 + [vspec()] * 4,
        out_specs=vspec(),
        compiler_params=params(),
        cost_estimate=cost(1 << 10, 1 << 20),
        name="halo_message",
    )(info, meta, *kv)


def movers_kernel(total, h, info, meta, *refs):
    qg, out = refs[:4], refs[4]

    def visit(s, c, rel, slot):
        @pl.when(rel >= 16)
        def _():
            out[cells(slot - 12), :] = qg[s][pl.ds(row_of(h)[s] + c * CELL, CELL), :]

    walk(meta, info[25], total, visit)


def movers_message(total, h, info, meta, qg):
    return pl.pallas_call(
        functools.partial(movers_kernel, total, h),
        out_shape=jax.ShapeDtypeStruct((2 * CELL, 128), F32),
        in_specs=[sspec()] * 2 + [vspec()] * 4,
        out_specs=vspec(),
        compiler_params=params(),
        cost_estimate=cost(1 << 10, 1 << 18),
        name="movers_message",
    )(info, meta, *qg)


def split(x):
    high = x.astype(BF16).astype(F32)
    return high, x - high


def nt(a, b):
    return lax.dot_general(a, b, (((1,), (1,)), ((), ())), preferred_element_type=F32)


def nn(a, b):
    return lax.dot_general(a, b, (((1,), (0,)), ((), ())), preferred_element_type=F32)


def tn(a, b):
    return lax.dot_general(a, b, (((0,), (0,)), ((), ())), preferred_element_type=F32)


def attend_kernel(total, h, info, meta, meta_prev, *refs):
    kv, halo, qg, qgm = refs[:4], refs[4], refs[5:9], refs[9]
    dkv, dq, back = refs[10:13]
    kcat, vcat, acc_k, acc_v, qcat, gcat, qrhs, grhs, s_scr, d_scr, dq_scr = refs[13:]
    start = info[25]
    start_prev = info[26]
    lane = lax.broadcasted_iota(jnp.int32, (CELL, 128), 1)
    row = lax.broadcasted_iota(jnp.int32, (CELL, 128), 0)
    low = lane < 64

    def put_key(x, slot, m, s, c):
        hidden = row >= m[s, 4 + c]
        for i in range(3):
            inside = (row >= 16 * (i + 1)) & (row < 16 * (i + 2))
            hidden = hidden | (inside & (m[s, 8 + 3 * c + i] > 0))
        bias = jnp.where(hidden & (lane == 64), NEGATIVE, 0.0)
        high, rest = split(x)
        high_r, rest_r = swap_half(high), swap_half(rest)
        mid, least = split(rest)
        kcat[cells(slot), pl.ds(0, 128)] = jnp.where(low, high, rest_r).astype(BF16)
        kcat[cells(slot), pl.ds(128, 128)] = jnp.where(low, high, bias).astype(BF16)
        kcat[cells(slot), pl.ds(256, 128)] = jnp.where(low, mid, swap_half(least)).astype(BF16)
        kcat[cells(slot), pl.ds(384, 128)] = jnp.where(low, high, 0.0).astype(BF16)
        vcat[cells(slot), pl.ds(0, 128)] = jnp.where(low, high_r, rest).astype(BF16)
        vcat[cells(slot), pl.ds(128, 128)] = jnp.where(low, high_r, 0.0).astype(BF16)

    one = jnp.where(lane == 64, 1.0, 0.0)

    def put_query(x, slot):
        high, rest = split(x)
        high_r, rest_r = swap_half(high), swap_half(rest)
        qcat[cells(slot), pl.ds(0, 128)] = jnp.where(low, high, high_r).astype(BF16)
        qcat[cells(slot), pl.ds(128, 128)] = jnp.where(low, rest, one).astype(BF16)
        mid, least = split(rest)
        qcat[cells(slot), pl.ds(256, 128)] = jnp.where(low, mid, high_r).astype(BF16)
        qcat[cells(slot), pl.ds(384, 128)] = jnp.where(low, least, 0.0).astype(BF16)
        gcat[cells(slot), pl.ds(0, 128)] = jnp.where(low, high_r, high).astype(BF16)
        gcat[cells(slot), pl.ds(128, 128)] = jnp.where(low, rest_r, 0.0).astype(BF16)
        qrhs[cells(slot), :] = jnp.where(low, high, rest_r).astype(BF16)
        grhs[cells(slot), :] = jnp.where(low, rest_r, high).astype(BF16)

    def own(s, c, rel, slot):
        @pl.when(rel < 16)
        def _():
            put_key(kv[s][pl.ds(row_of(h)[s] + c * CELL, CELL), :], 12 + rel, meta, s, c)
            put_query(qg[s][pl.ds(row_of(h)[s] + c * CELL, CELL), :], rel)

    walk(meta, start, total, own)

    def before(s, c, rel, slot):
        @pl.when(rel >= 4)
        def _():
            put_key(halo[cells(slot), :], rel - 4, meta_prev, s, c)

        @pl.when(rel >= 16)
        def _():
            put_query(qgm[cells(slot - 12), :], rel - 16)

    walk(meta_prev, start_prev, total, before)
    acc_k[...] = jnp.zeros(acc_k.shape, F32)
    acc_v[...] = jnp.zeros(acc_v.shape, F32)

    def fold(x, op):
        out = x[0:8]
        for i in range(1, ROWS // 8):
            out = op(out, x[8 * i : 8 * i + 8])
        return out

    def block(b, carry):
        q_rows = pl.ds(pl.multiple_of(b * ROWS, ROWS), ROWS)

        def k_rows(c):
            return pl.ds(pl.multiple_of((b + c) * ROWS, ROWS), ROWS)

        top = None
        for c in range(4):
            scores = nt(kcat[k_rows(c), :], qcat[q_rows, :])
            s_scr[pl.ds(c * ROWS, ROWS), :] = scores
            part = fold(scores, jnp.maximum)
            top = part if top is None else jnp.maximum(top, part)
        top = jnp.max(top, axis=0, keepdims=True)
        size = jnp.zeros((8, ROWS), F32)
        dots = jnp.zeros((8, ROWS), F32)
        for c in range(4):
            weights = jnp.exp(s_scr[pl.ds(c * ROWS, ROWS), :] - top)
            grad_weights = nt(vcat[k_rows(c), :], gcat[q_rows, :])
            s_scr[pl.ds(c * ROWS, ROWS), :] = weights
            d_scr[pl.ds(c * ROWS, ROWS), :] = grad_weights
            size = size + fold(weights, jnp.add)
            dots = dots + fold(weights * grad_weights, jnp.add)
        inverse = 1.0 / jnp.sum(size, axis=0, keepdims=True)
        delta = jnp.sum(dots, axis=0, keepdims=True) * inverse
        dq_t = jnp.zeros((128, ROWS), F32)
        for c in range(4):
            weights = s_scr[pl.ds(c * ROWS, ROWS), :] * inverse
            grad_scores = weights * (d_scr[pl.ds(c * ROWS, ROWS), :] - delta)
            high = weights.astype(BF16)
            rest = (weights - high.astype(F32)).astype(BF16)
            acc_v[k_rows(c), :] += nn(high, grhs[q_rows, :]) + nn(rest, grhs[q_rows, :])
            high = grad_scores.astype(BF16)
            rest = (grad_scores - high.astype(F32)).astype(BF16)
            acc_k[k_rows(c), :] += nn(high, qrhs[q_rows, :]) + nn(rest, qrhs[q_rows, :])
            keys = kcat[k_rows(c), pl.ds(0, 128)]
            dq_t = dq_t + tn(keys, high) + tn(keys, rest)
        dq_t = (dq_t[0:64] + dq_t[64:128]) * SCALE
        dq_scr[q_rows, :] = jnp.concatenate([dq_t, dq_t], axis=0).T
        return carry

    lax.fori_loop(0, 4, block, 0)

    def grad_kv(slot):
        a = acc_k[cells(slot), :]
        b = acc_v[cells(slot), :]
        return jnp.where(low, a + swap_half(a), b + swap_half(b))

    def own_out(s, c, rel, slot):
        here = rel < 16
        x = grad_kv(jnp.where(here, 12 + rel, 0))
        dkv[pl.ds(s * ROWS + c * CELL, CELL), :] = jnp.where(here, x, 0.0)
        x = dq_scr[cells(jnp.where(here, rel, 0)), :]
        half = pl.ds(s * 128 + (c // 2) * CELL, CELL)
        if c % 2 == 0:
            dq[half, :] = x
        else:
            dq[half, :] = jnp.where(low, dq[half, :], x)

    walk(meta, start, total, own_out)
    pair = pl.ds(HALO * CELL, CELL)

    def before_out(s, c, rel, slot):
        @pl.when(rel >= 4)
        def _():
            back[cells(slot), :] = grad_kv(rel - 4)

        @pl.when(rel >= 16)
        def _():
            x = dq_scr[cells(rel - 16), :]
            first = slot == 12
            back[pair, :] = jnp.where(low == first, x, back[pair, :])

    walk(meta_prev, start_prev, total, before_out)


def attend(total, h, info, meta, meta_prev, kv, halo, qg, qgm):
    shapes = [(4 * ROWS, 128), (2 * ROWS, 128), (HALO * CELL + CELL, 128)]
    keys, queries = 28 * CELL, 16 * CELL
    return pl.pallas_call(
        functools.partial(attend_kernel, total, h),
        out_shape=[jax.ShapeDtypeStruct(s, F32) for s in shapes],
        in_specs=[sspec()] * 3 + [vspec()] * 10,
        out_specs=[vspec()] * 3,
        scratch_shapes=[
            VMEM((keys, 512), BF16),
            VMEM((keys, 256), BF16),
            VMEM((keys, 128), F32),
            VMEM((keys, 128), F32),
            VMEM((queries, 512), BF16),
            VMEM((queries, 256), BF16),
            VMEM((queries, 128), BF16),
            VMEM((queries, 128), BF16),
            VMEM((4 * ROWS, ROWS), F32),
            VMEM((4 * ROWS, ROWS), F32),
            VMEM((queries, 128), F32),
        ],
        compiler_params=params(24),
        cost_estimate=cost(8 << 30, 8 << 20),
        name="attend",
    )(info, meta, meta_prev, *kv, halo, *qg, qgm)


OUT = ROWS + ROWS // 2


def finish_kernel(total, info, meta, dkv, dq, back, *outs):
    low = lanes((CELL, 128)) < 64
    pair = back[pl.ds(HALO * CELL, CELL), :]
    for s in range(PLANE):
        outs[s][pl.ds(ROWS, 128), :] = dq[pl.ds(s * 128, 128), :]

    def visit(s, c, rel, slot):
        out = outs[s]
        sent = rel >= 4
        x = jnp.where(sent, back[cells(jnp.where(sent, slot, 0)), :], 0.0)
        out[pl.ds(c * CELL, CELL), :] = dkv[pl.ds(s * ROWS + c * CELL, CELL), :] + x

        @pl.when(rel >= 16)
        def _():
            straight = (slot - 12) == (c % 2)
            x = jnp.where(straight, pair, swap_half(pair))
            half = pl.ds(ROWS + (c // 2) * CELL, CELL)
            out[half, :] = jnp.where(low == (c % 2 == 0), x, out[half, :])

    walk(meta, info[25], total, visit)


def finish(total, info, meta, dkv, dq, back):
    shapes = [(OUT, 128)] * 4
    return pl.pallas_call(
        functools.partial(finish_kernel, total),
        out_shape=[jax.ShapeDtypeStruct(s, F32) for s in shapes],
        in_specs=[sspec()] * 2 + [vspec()] * 3,
        out_specs=[vspec()] * 4,
        compiler_params=params(),
        cost_estimate=cost(1 << 10, 2 << 20),
        name="finish",
    )(info, meta, dkv, dq, back)


def unpack_kernel(info, *refs):
    parts, (oq, ok, ov) = refs[:12], refs[12:]
    me = info[24]

    def grads(s, c, h):
        return parts[4 * h + s][pl.ds(c * CELL, CELL), :]

    def query(s, c, h):
        x = parts[4 * h + s][pl.ds(ROWS + (c // 2) * CELL, CELL), :]
        return x, swap_half(x)

    for s in range(PLANE):
        j = lax.bitwise_xor(me, s)
        first = pl.ds(pl.multiple_of(j * 128, 128), 128)
        for c in range(CELLS):
            r = pl.ds(c * CELL, CELL)
            a, b = grads(s, c, 0), grads(s, c, 1)
            ok[r, first] = join(a, swap_half(b))
            ov[r, first] = join(swap_half(a), b)
            x0, y0 = query(s, c, 0)
            x1, y1 = query(s, c, 1)
            oq[r, first] = join(x0, y1) if c % 2 == 0 else join(y0, x1)
    for s in (0, 2):
        j = lax.bitwise_xor(me, s)
        even = (j % 2) == 0
        last = pl.ds(pl.multiple_of((4 + j // 2) * 128, 128), 128)
        for c in range(CELLS):
            r = pl.ds(c * CELL, CELL)
            u, w = grads(s, c, 2), grads(s + 1, c, 2)
            a, b = jnp.where(even, u, w), jnp.where(even, w, u)
            ok[r, last] = join(a, swap_half(b))
            ov[r, last] = join(swap_half(a), b)
            u, w = query(s, c, 2)[0], query(s + 1, c, 2)[0]
            a, b = jnp.where(even, u, w), jnp.where(even, w, u)
            oq[r, last] = join(a, swap_half(b)) if c % 2 == 0 else join(swap_half(a), b)


def unpack_heads(info, parts, features):
    return pl.pallas_call(
        unpack_kernel,
        out_shape=[jax.ShapeDtypeStruct((ROWS, features), F32)] * 3,
        in_specs=[sspec()] + [vspec()] * 12,
        out_specs=[vspec()] * 3,
        compiler_params=params(),
        cost_estimate=cost(1 << 20, 5 << 20),
        name="unpack_heads",
    )(info, *[x for part in parts for x in part])


def after(x, *earlier):
    return lax.optimization_barrier((x, *earlier))[0]


def on_device(query_rows, key_rows, value_rows, grad_rows, placement, cell_lengths, gene_mask):
    count = lax.axis_size("ctx")
    total = count * CELLS
    index = lax.axis_index("ctx").astype(jnp.int32)
    plane = index // PLANE

    def along_z(x, step):
        return lax.ppermute(x, "ctx", [(i, (i + step * PLANE) % count) for i in range(count)])

    def swap(x, bit):
        return lax.ppermute(x, "ctx", [(i, i ^ bit) for i in range(count)])

    start = plane * (PLANE * CELLS)
    start_prev = lax.rem(start - PLANE * CELLS + total, total)
    tail = jnp.stack([jnp.int32(0)] * 4 + [index % PLANE, start, start_prev, jnp.int32(0)])
    info = jnp.concatenate([placement, cell_lengths, gene_mask.reshape(-1), tail])

    kv_mine, kv_core, *kv_y = pack_heads(plain, True, info, key_rows, value_rows)

    def across(parts, h, *earlier):
        return [swap(after(parts[2 * h + i], *earlier), 2 + i) for i in range(2)]

    kv0 = across(kv_y, 0)
    kv_core = swap(kv_core, 1)
    qg_mine, qg_core, *qg_y = pack_heads(scaled, False, after(info, kv_mine), query_rows, grad_rows)
    qg0 = across(qg_y, 0)
    kv0 = list(after(tuple(kv0), qg_mine))
    kv1 = across(kv_y, 1, *kv0)
    kv = [(kv_mine, kv_core, *kv0)]
    meta = jnp.stack([x[r, :32] for x, r in zip(kv[0], META_ROWS)]).astype(jnp.int32)
    halo = [along_z(halo_message(total, 0, info, meta, kv[0]), 1)]
    qg_core = swap(after(qg_core, kv_core), 1)
    qg = [(qg_mine, qg_core, *qg0)]
    qgm = [along_z(movers_message(total, 0, info, meta, qg[0]), 1)]
    kv2 = across(kv_y, 2, *qg0)
    kv.append((kv_mine, kv_core, *kv1))
    halo.append(along_z(halo_message(total, 1, info, meta, kv[1]), 1))
    qg1 = across(qg_y, 1, *kv1)
    kv.append((kv_mine, kv_core, *kv2))
    halo.append(along_z(halo_message(total, 2, info, meta, kv[2]), 1))
    qg2 = across(qg_y, 2, *kv2)
    for y in (qg1, qg2):
        qg.append((qg_mine, qg_core, *y))
        qgm.append(along_z(movers_message(total, len(qg) - 1, info, meta, qg[-1]), 1))
    meta_prev = halo[0][HALO * CELL : HALO * CELL + 4, :32].astype(jnp.int32)

    parts = []
    turn = ()
    for h in range(HEADS):
        late = after(qgm[h], *turn)
        dkv, dq, back = attend(total, h, info, meta, meta_prev, kv[h], halo[h], qg[h], late)
        turn = (dq,)
        mine, *outs = finish(total, info, meta, dkv, dq, along_z(back, -1))
        parts.append([mine] + [swap(x, i + 1) for i, x in enumerate(outs)])
    return tuple(unpack_heads(info, parts, query_rows.shape[1]))


def solution(mesh):
    rows = P(("groups", "ctx"), None)
    flat = P(("groups", "ctx"))
    return jax.shard_map(
        on_device,
        mesh=mesh,
        in_specs=(rows, rows, rows, rows, flat, flat, rows),
        out_specs=(rows, rows, rows),
        check_vma=False,
    )
```

profile of v0, /device:TPU:1, one launch (start us, length us, event | category | flops | bytes accessed | tf_op | source)
XLA Modules:
  0.0 136.1 jit_solution(3889668553265372366)
XLA Ops:
  0.7 0.7 copy-done.4
  1.3 0.1 reshape.9
  1.4 0.7 copy-done.5
  2.1 0.0 copy-done.6
  2.1 0.1 concatenate.3.info
  2.2 1.1 copy-done
  3.3 1.1 copy-done.1
  4.4 3.5 %pack_heads.2 = (f32[776,128]{1,0:T(8,128)S(1)}, f32[776,128]{1,0:T(8,128)S(1)}, f32[264,128]{1,0:T(8,128)S(1)}, f32[264,128]{1,0:T(8,128)S(1)}, f32[256,128]{1,...) custom-call(s32[28]{0:T(128)S(1)} %concatenate.3.info, ...), custom_call_target="tpu_custom_call" | custom-call | flops 1048576 | bytes 3145728 | tf_op jit(solution)/shard_map/pack_heads/pallas_call | solution.py:110
  7.9 0.1 collective-permute-start
  8.1 2.7 %collective-permute-start.1 = (f32[264,128]{1,0:T(8,128)S(1)}, f32[264,128]{1,0:T(8,128)S(1)}, u32[]{:S(2)}, u32[]{:S(2)}) collective-permute-start(f32[264,128]{1,0:T(8,128)S(1)} %get-tuple-element.56), channel_id=1, source_target_pairs={{0,2},{1,3},{2,0},{3,1},{4,6},{5,7},{6,4},{7,5},{8,10},{9,11},{10,... | collective-permute-start | bytes 405512 | tf_op jit(solution)/shard_map/ppermute | solution.py:483
  10.8 0.0 collective-permute-start.2
  10.8 3.5 %pack_heads.3 = (f32[768,128]{1,0:T(8,128)S(1)}, f32[768,128]{1,0:T(8,128)S(1)}, f32[256,128]{1,0:T(8,128)S(1)}, f32[256,128]{1,0:T(8,128)S(1)}, f32[256,128]{1,...) custom-call(s32[28]{0:T(128)S(1)} %concatenate.3.info, ...), custom_call_target="tpu_custom_call" | custom-call | flops 1048576 | bytes 3145728 | tf_op jit(solution)/shard_map/pack_heads/pallas_call | solution.py:110
  14.3 0.3 collective-permute-done.1.refs_2_
  14.6 2.9 %collective-permute-done.2.refs_3_ = f32[264,128]{1,0:T(8,128)S(1)} collective-permute-done((f32[264,128]{1,0:T(8,128)S(1)}, f32[264,128]{1,0:T(8,128)S(1)}, u32[]{:S(2)}, u32[]{:S(2)}) %collective-permute-start.2) | collective-permute-done | bytes 135200 | tf_op jit(solution)/shard_map/ppermute | solution.py:483
  17.5 0.5 collective-permute-start.4
  18.0 0.8 halo_message.3
  18.8 1.4 %collective-permute-start.3 = (f32[904,128]{1,0:T(8,128)S(1)}, f32[904,128]{1,0:T(8,128)S(1)}, u32[]{:S(2)}, u32[]{:S(2)}) collective-permute-start(f32[904,128]{1,0:T(8,128)S(1)} %halo_message.3), channel_id=1, source_target_pairs={{0,4},{1,5},{2,6},{3,7},{4,8},{5,9},{6,10},{7,11},{8,12},{9,13},{1... | collective-permute-start | bytes 1388552 | tf_op jit(solution)/shard_map/ppermute | solution.py:480
  20.2 1.2 collective-permute-start.5
  21.4 0.9 collective-permute-start.6
  22.4 1.2 collective-permute-start.12
  23.6 1.1 collective-permute-done.5.refs_2_.refs_7_
  24.7 3.6 %collective-permute-start.13 = (f32[256,128]{1,0:T(8,128)S(1)}, f32[256,128]{1,0:T(8,128)S(1)}, u32[]{:S(2)}, u32[]{:S(2)}) collective-permute-start(f32[256,128]{1,0:T(8,128)S(1)} %get-tuple-element.76), channel_id=1, source_target_pairs={{0,3},{1,2},{2,1},{3,0},{4,7},{5,6},{6,5},{7,4},{8,11},{9,10},{10,... | collective-permute-start | bytes 393224 | tf_op jit(solution)/shard_map/ppermute | solution.py:483
  28.2 1.1 collective-permute-done.6.refs_3_.refs_8_
  29.4 1.4 %collective-permute-start.22 = (f32[256,128]{1,0:T(8,128)S(1)}, f32[256,128]{1,0:T(8,128)S(1)}, u32[]{:S(2)}, u32[]{:S(2)}) collective-permute-start(f32[256,128]{1,0:T(8,128)S(1)} %get-tuple-element.90), channel_id=1, source_target_pairs={{0,2},{1,3},{2,0},{3,1},{4,6},{5,7},{6,4},{7,5},{8,10},{9,11},{10,... | collective-permute-start | bytes 393224 | tf_op jit(solution)/shard_map/ppermute | solution.py:483
  30.8 3.1 %collective-permute-start.23 = (f32[256,128]{1,0:T(8,128)S(1)}, f32[256,128]{1,0:T(8,128)S(1)}, u32[]{:S(2)}, u32[]{:S(2)}) collective-permute-start(f32[256,128]{1,0:T(8,128)S(1)} %get-tuple-element.92), channel_id=1, source_target_pairs={{0,3},{1,2},{2,1},{3,0},{4,7},{5,6},{6,5},{7,4},{8,11},{9,10},{10,... | collective-permute-start | bytes 393224 | tf_op jit(solution)/shard_map/ppermute | solution.py:483
  33.8 0.8 collective-permute-done.13.refs_3_
  34.7 1.4 %collective-permute-start.15 = (f32[256,128]{1,0:T(8,128)S(1)}, f32[256,128]{1,0:T(8,128)S(1)}, u32[]{:S(2)}, u32[]{:S(2)}) collective-permute-start(f32[256,128]{1,0:T(8,128)S(1)} %get-tuple-element.78), channel_id=1, source_target_pairs={{0,2},{1,3},{2,0},{3,1},{4,6},{5,7},{6,4},{7,5},{8,10},{9,11},{10,... | collective-permute-start | bytes 393224 | tf_op jit(solution)/shard_map/ppermute | solution.py:483
  36.1 4.2 %collective-permute-done.23.refs_3_ = f32[256,128]{1,0:T(8,128)S(1)} collective-permute-done((f32[256,128]{1,0:T(8,128)S(1)}, f32[256,128]{1,0:T(8,128)S(1)}, u32[]{:S(2)}, u32[]{:S(2)}) %collective-permute-start.23) | collective-permute-done | bytes 131104 | tf_op jit(solution)/shard_map/ppermute | solution.py:483
  40.3 1.4 %collective-permute-start.25 = (f32[256,128]{1,0:T(8,128)S(1)}, f32[256,128]{1,0:T(8,128)S(1)}, u32[]{:S(2)}, u32[]{:S(2)}) collective-permute-start(f32[256,128]{1,0:T(8,128)S(1)} %get-tuple-element.94), channel_id=1, source_target_pairs={{0,2},{1,3},{2,0},{3,1},{4,6},{5,7},{6,4},{7,5},{8,10},{9,11},{10,... | collective-permute-start | bytes 393224 | tf_op jit(solution)/shard_map/ppermute | solution.py:483
  41.7 0.1 collective-permute-start.16
  41.8 1.6 %collective-permute-start.26 = (f32[256,128]{1,0:T(8,128)S(1)}, f32[256,128]{1,0:T(8,128)S(1)}, u32[]{:S(2)}, u32[]{:S(2)}) collective-permute-start(f32[256,128]{1,0:T(8,128)S(1)} %get-tuple-element.96), channel_id=1, source_target_pairs={{0,3},{1,2},{2,1},{3,0},{4,7},{5,6},{6,5},{7,4},{8,11},{9,10},{10,... | collective-permute-start | bytes 393224 | tf_op jit(solution)/shard_map/ppermute | solution.py:483
  43.4 0.8 movers_message.3
  44.2 1.3 collective-permute-start.7
  45.6 0.8 halo_message.4
  46.3 0.8 halo_message.5
  47.1 1.8 %collective-permute-done.16.refs_3_.refs_8_ = f32[256,128]{1,0:T(8,128)S(1)} collective-permute-done((f32[256,128]{1,0:T(8,128)S(1)}, f32[256,128]{1,0:T(8,128)S(1)}, u32[]{:S(2)}, u32[]{:S(2)}) %collective-permute-start.16) | collective-permute-done | bytes 131104 | tf_op jit(solution)/shard_map/ppermute | solution.py:483
  48.9 1.3 collective-permute-start.14
  50.2 0.8 movers_message.4
  50.9 1.3 collective-permute-start.24
  52.3 0.2 collective-permute-start.17
  52.5 0.8 movers_message.5
  53.2 1.3 collective-permute-start.27
  54.6 13.4 %attend.3 = (f32[1024,128]{1,0:T(8,128)S(1)}, f32[512,128]{1,0:T(8,128)S(1)}, f32[960,128]{1,0:T(8,128)S(1)}) custom-call(s32[28]{0:T(128)S(1)} %concatenate.3.info, s32[4,32]{1,0:T(4,128)S(1)} %maximum_convert_fusion.meta, s32[4,32]{1,0:T(4,128)S(1)} %slice_convert_fusion.meta_prev, f32[776,128]{1,0:T(8,128)S(1)} %get-tuple-element.54.refs_0_, ...), custom_call_target="tpu_custom_call" | custom-call | flops 8589934592 | bytes 8388608 | tf_op jit(solution)/shard_map/attend/pallas_call | solution.py:358
  68.0 2.0 %collective-permute-start.8 = (f32[960,128]{1,0:T(8,128)S(1)}, f32[960,128]{1,0:T(8,128)S(1)}, u32[]{:S(2)}, u32[]{:S(2)}) collective-permute-start(f32[960,128]{1,0:T(8,128)S(1)} %get-tuple-element.68), channel_id=1, source_target_pairs={{0,12},{1,13},{2,14},{3,15},{4,0},{5,1},{6,2},{7,3},{8,4},{9,5},{1... | collective-permute-start | bytes 1474568 | tf_op jit(solution)/shard_map/ppermute | solution.py:480
  70.1 4.1 %collective-permute-done.17.refs_9_ = f32[128,128]{1,0:T(8,128)S(1)} collective-permute-done((f32[128,128]{1,0:T(8,128)S(1)}, f32[128,128]{1,0:T(8,128)S(1)}, u32[]{:S(2)}, u32[]{:S(2)}) %collective-permute-start.17) | collective-permute-done | bytes 65568 | tf_op jit(solution)/shard_map/ppermute | solution.py:480
  74.1 13.6 %attend.4 = (f32[1024,128]{1,0:T(8,128)S(1)}, f32[512,128]{1,0:T(8,128)S(1)}, f32[960,128]{1,0:T(8,128)S(1)}) custom-call(s32[28]{0:T(128)S(1)} %concatenate.3.info, s32[4,32]{1,0:T(4,128)S(1)} %maximum_convert_fusion.meta, s32[4,32]{1,0:T(4,128)S(1)} %slice_convert_fusion.meta_prev, f32[776,128]{1,0:T(8,128)S(1)} %get-tuple-element.54.refs_0_, ...), custom_call_target="tpu_custom_call" | custom-call | flops 8589934592 | bytes 8388608 | tf_op jit(solution)/shard_map/attend/pallas_call | solution.py:358
  87.8 0.3 collective-permute-start.18
  88.1 13.4 %attend.5 = (f32[1024,128]{1,0:T(8,128)S(1)}, f32[512,128]{1,0:T(8,128)S(1)}, f32[960,128]{1,0:T(8,128)S(1)}) custom-call(s32[28]{0:T(128)S(1)} %concatenate.3.info, s32[4,32]{1,0:T(4,128)S(1)} %maximum_convert_fusion.meta, s32[4,32]{1,0:T(4,128)S(1)} %slice_convert_fusion.meta_prev, f32[776,128]{1,0:T(8,128)S(1)} %get-tuple-element.54.refs_0_, ...), custom_call_target="tpu_custom_call" | custom-call | flops 8589934592 | bytes 8388608 | tf_op jit(solution)/shard_map/attend/pallas_call | solution.py:358
  101.5 1.4 %collective-permute-start.28 = (f32[960,128]{1,0:T(8,128)S(1)}, f32[960,128]{1,0:T(8,128)S(1)}, u32[]{:S(2)}, u32[]{:S(2)}) collective-permute-start(f32[960,128]{1,0:T(8,128)S(1)} %get-tuple-element.100), channel_id=1, source_target_pairs={{0,12},{1,13},{2,14},{3,15},{4,0},{5,1},{6,2},{7,3},{8,4},{9,5},{1... | collective-permute-start | bytes 1474568 | tf_op jit(solution)/shard_map/ppermute | solution.py:480
  103.0 0.9 finish.3
  103.9 1.7 %collective-permute-start.9 = (f32[384,128]{1,0:T(8,128)S(1)}, f32[384,128]{1,0:T(8,128)S(1)}, u32[]{:S(2)}, u32[]{:S(2)}) collective-permute-start(f32[384,128]{1,0:T(8,128)S(1)} %get-tuple-element.70), channel_id=1, source_target_pairs={{0,1},{1,0},{2,3},{3,2},{4,5},{5,4},{6,7},{7,6},{8,9},{9,8},{10,11... | collective-permute-start | bytes 589832 | tf_op jit(solution)/shard_map/ppermute | solution.py:483
  105.6 1.6 %collective-permute-start.10 = (f32[384,128]{1,0:T(8,128)S(1)}, f32[384,128]{1,0:T(8,128)S(1)}, u32[]{:S(2)}, u32[]{:S(2)}) collective-permute-start(f32[384,128]{1,0:T(8,128)S(1)} %get-tuple-element.71), channel_id=1, source_target_pairs={{0,2},{1,3},{2,0},{3,1},{4,6},{5,7},{6,4},{7,5},{8,10},{9,11},{10,... | collective-permute-start | bytes 589832 | tf_op jit(solution)/shard_map/ppermute | solution.py:483
  107.3 0.1 collective-permute-start.11
  107.3 0.9 finish.4
  108.3 0.4 collective-permute-start.19
  108.7 4.4 %collective-permute-done.28.back = f32[960,128]{1,0:T(8,128)S(1)} collective-permute-done((f32[960,128]{1,0:T(8,128)S(1)}, f32[960,128]{1,0:T(8,128)S(1)}, u32[]{:S(2)}, u32[]{:S(2)}) %collective-permute-start.28) | collective-permute-done | bytes 491552 | tf_op jit(solution)/shard_map/ppermute | solution.py:480
  113.1 0.9 finish.5
  114.1 3.8 %collective-permute-start.21 = (f32[384,128]{1,0:T(8,128)S(1)}, f32[384,128]{1,0:T(8,128)S(1)}, u32[]{:S(2)}, u32[]{:S(2)}) collective-permute-start(f32[384,128]{1,0:T(8,128)S(1)} %get-tuple-element.88), channel_id=1, source_target_pairs={{0,3},{1,2},{2,1},{3,0},{4,7},{5,6},{6,5},{7,4},{8,11},{9,10},{10,... | collective-permute-start | bytes 589832 | tf_op jit(solution)/shard_map/ppermute | solution.py:483
  117.9 0.7 collective-permute-start.30
  118.5 1.5 %collective-permute-start.31 = (f32[384,128]{1,0:T(8,128)S(1)}, f32[384,128]{1,0:T(8,128)S(1)}, u32[]{:S(2)}, u32[]{:S(2)}) collective-permute-start(f32[384,128]{1,0:T(8,128)S(1)} %get-tuple-element.104), channel_id=1, source_target_pairs={{0,3},{1,2},{2,1},{3,0},{4,7},{5,6},{6,5},{7,4},{8,11},{9,10},{10,... | collective-permute-start | bytes 589832 | tf_op jit(solution)/shard_map/ppermute | solution.py:483
  120.0 6.6 %collective-permute-done.21.refs_7_ = f32[384,128]{1,0:T(8,128)S(1)} collective-permute-done((f32[384,128]{1,0:T(8,128)S(1)}, f32[384,128]{1,0:T(8,128)S(1)}, u32[]{:S(2)}, u32[]{:S(2)}) %collective-permute-start.21) | collective-permute-done | bytes 196640 | tf_op jit(solution)/shard_map/ppermute | solution.py:483
  126.6 1.8 %collective-permute-done.30.refs_10_ = f32[384,128]{1,0:T(8,128)S(1)} collective-permute-done((f32[384,128]{1,0:T(8,128)S(1)}, f32[384,128]{1,0:T(8,128)S(1)}, u32[]{:S(2)}, u32[]{:S(2)}) %collective-permute-start.30) | collective-permute-done | bytes 196640 | tf_op jit(solution)/shard_map/ppermute | solution.py:483
  128.4 5.1 %collective-permute-done.31.refs_11_ = f32[384,128]{1,0:T(8,128)S(1)} collective-permute-done((f32[384,128]{1,0:T(8,128)S(1)}, f32[384,128]{1,0:T(8,128)S(1)}, u32[]{:S(2)}, u32[]{:S(2)}) %collective-permute-start.31) | collective-permute-done | bytes 196640 | tf_op jit(solution)/shard_map/ppermute | solution.py:483
  133.5 2.6 %unpack_heads.1 = (f32[256,768]{1,0:T(8,128)}, f32[256,768]{1,0:T(8,128)}, f32[256,768]{1,0:T(8,128)}) custom-call(s32[28]{0:T(128)S(1)} %concatenate.3.info, f32[384,128]{1,0:T(8,128)S(1)} %get-tuple-element.69.refs_0_, f32[384,128]{1,0:T(8,128)S(1)} %collective-permute-done.9.refs_1_, f32[384,128]{1,0:T(8,128)S(1)} %collective-permute-done.10.refs_2_, ...), custom_call_target="tpu_custom_call" | custom-call | flops 1048576 | bytes 5242880 | tf_op jit(solution)/shard_map/unpack_heads/pallas_call | solution.py:458
  (38 shorter events, 0.1 us)
Async XLA Ops:
  0.7 0.7 copy-start.4
  1.4 0.7 copy-start.5
  1.4 0.7 copy-start.6
  2.2 1.1 copy-start
  3.3 1.1 copy-start.1
  4.4 6.4 %copy-start.2 = (f32[256,768]{1,0:T(8,128)S(1)}, f32[256,768]{1,0:T(8,128)}, u32[]{:S(2)}) copy-start(f32[256,768]{1,0:T(8,128)} %a_hbm.3) | copy-start | bytes 2359300
  4.4 6.4 %copy-start.3 = (f32[256,768]{1,0:T(8,128)S(1)}, f32[256,768]{1,0:T(8,128)}, u32[]{:S(2)}) copy-start(f32[256,768]{1,0:T(8,128)} %b_hbm.3) | copy-start | bytes 2359300
  7.9 9.6 %collective-permute-start = (f32[776,128]{1,0:T(8,128)S(1)}, f32[776,128]{1,0:T(8,128)S(1)}, u32[]{:S(2)}, u32[]{:S(2)}) collective-permute-start(f32[776,128]{1,0:T(8,128)S(1)} %get-tuple-element.55), channel_id=1, source_target_pairs={{0,1},{1,0},{2,3},{3,2},{4,5},{5,4},{6,7},{7,6},{8,9},{9,8},{10,11... | collective-permute-start | bytes 1191944 | tf_op jit(solution)/shard_map/ppermute | solution.py:483
  8.1 6.6 %collective-permute-start.1 = (f32[264,128]{1,0:T(8,128)S(1)}, f32[264,128]{1,0:T(8,128)S(1)}, u32[]{:S(2)}, u32[]{:S(2)}) collective-permute-start(f32[264,128]{1,0:T(8,128)S(1)} %get-tuple-element.56), channel_id=1, source_target_pairs={{0,2},{1,3},{2,0},{3,1},{4,6},{5,7},{6,4},{7,5},{8,10},{9,11},{10,... | collective-permute-start | bytes 405512 | tf_op jit(solution)/shard_map/ppermute | solution.py:483
  10.8 6.8 %collective-permute-start.2 = (f32[264,128]{1,0:T(8,128)S(1)}, f32[264,128]{1,0:T(8,128)S(1)}, u32[]{:S(2)}, u32[]{:S(2)}) collective-permute-start(f32[264,128]{1,0:T(8,128)S(1)} %get-tuple-element.57), channel_id=1, source_target_pairs={{0,3},{1,2},{2,1},{3,0},{4,7},{5,6},{6,5},{7,4},{8,11},{9,10},{10,... | collective-permute-start | bytes 405512 | tf_op jit(solution)/shard_map/ppermute | solution.py:483
  17.5 24.3 %collective-permute-start.4 = (f32[768,128]{1,0:T(8,128)S(1)}, f32[768,128]{1,0:T(8,128)S(1)}, u32[]{:S(2)}, u32[]{:S(2)}) collective-permute-start(f32[768,128]{1,0:T(8,128)S(1)} %get-tuple-element.63), channel_id=1, source_target_pairs={{0,1},{1,0},{2,3},{3,2},{4,5},{5,4},{6,7},{7,6},{8,9},{9,8},{10,11... | collective-permute-start | bytes 1179656 | tf_op jit(solution)/shard_map/ppermute | solution.py:483
  18.8 35.8 %collective-permute-start.3 = (f32[904,128]{1,0:T(8,128)S(1)}, f32[904,128]{1,0:T(8,128)S(1)}, u32[]{:S(2)}, u32[]{:S(2)}) collective-permute-start(f32[904,128]{1,0:T(8,128)S(1)} %halo_message.3), channel_id=1, source_target_pairs={{0,4},{1,5},{2,6},{3,7},{4,8},{5,9},{6,10},{7,11},{8,12},{9,13},{1... | collective-permute-start | bytes 1388552 | tf_op jit(solution)/shard_map/ppermute | solution.py:480
  20.2 4.5 %collective-permute-start.5 = (f32[256,128]{1,0:T(8,128)S(1)}, f32[256,128]{1,0:T(8,128)S(1)}, u32[]{:S(2)}, u32[]{:S(2)}) collective-permute-start(f32[256,128]{1,0:T(8,128)S(1)} %get-tuple-element.64), channel_id=1, source_target_pairs={{0,2},{1,3},{2,0},{3,1},{4,6},{5,7},{6,4},{7,5},{8,10},{9,11},{10,... | collective-permute-start | bytes 393224 | tf_op jit(solution)/shard_map/ppermute | solution.py:483
  21.4 7.9 %collective-permute-start.6 = (f32[256,128]{1,0:T(8,128)S(1)}, f32[256,128]{1,0:T(8,128)S(1)}, u32[]{:S(2)}, u32[]{:S(2)}) collective-permute-start(f32[256,128]{1,0:T(8,128)S(1)} %get-tuple-element.65), channel_id=1, source_target_pairs={{0,3},{1,2},{2,1},{3,0},{4,7},{5,6},{6,5},{7,4},{8,11},{9,10},{10,... | collective-permute-start | bytes 393224 | tf_op jit(solution)/shard_map/ppermute | solution.py:483
  22.4 8.4 %collective-permute-start.12 = (f32[256,128]{1,0:T(8,128)S(1)}, f32[256,128]{1,0:T(8,128)S(1)}, u32[]{:S(2)}, u32[]{:S(2)}) collective-permute-start(f32[256,128]{1,0:T(8,128)S(1)} %get-tuple-element.74), channel_id=1, source_target_pairs={{0,2},{1,3},{2,0},{3,1},{4,6},{5,7},{6,4},{7,5},{8,10},{9,11},{10,... | collective-permute-start | bytes 393224 | tf_op jit(solution)/shard_map/ppermute | solution.py:483
  24.7 10.0 %collective-permute-start.13 = (f32[256,128]{1,0:T(8,128)S(1)}, f32[256,128]{1,0:T(8,128)S(1)}, u32[]{:S(2)}, u32[]{:S(2)}) collective-permute-start(f32[256,128]{1,0:T(8,128)S(1)} %get-tuple-element.76), channel_id=1, source_target_pairs={{0,3},{1,2},{2,1},{3,0},{4,7},{5,6},{6,5},{7,4},{8,11},{9,10},{10,... | collective-permute-start | bytes 393224 | tf_op jit(solution)/shard_map/ppermute | solution.py:483
  29.4 6.7 %collective-permute-start.22 = (f32[256,128]{1,0:T(8,128)S(1)}, f32[256,128]{1,0:T(8,128)S(1)}, u32[]{:S(2)}, u32[]{:S(2)}) collective-permute-start(f32[256,128]{1,0:T(8,128)S(1)} %get-tuple-element.90), channel_id=1, source_target_pairs={{0,2},{1,3},{2,0},{3,1},{4,6},{5,7},{6,4},{7,5},{8,10},{9,11},{10,... | collective-permute-start | bytes 393224 | tf_op jit(solution)/shard_map/ppermute | solution.py:483
  30.8 9.5 %collective-permute-start.23 = (f32[256,128]{1,0:T(8,128)S(1)}, f32[256,128]{1,0:T(8,128)S(1)}, u32[]{:S(2)}, u32[]{:S(2)}) collective-permute-start(f32[256,128]{1,0:T(8,128)S(1)} %get-tuple-element.92), channel_id=1, source_target_pairs={{0,3},{1,2},{2,1},{3,0},{4,7},{5,6},{6,5},{7,4},{8,11},{9,10},{10,... | collective-permute-start | bytes 393224 | tf_op jit(solution)/shard_map/ppermute | solution.py:483
  34.7 9.5 %collective-permute-start.15 = (f32[256,128]{1,0:T(8,128)S(1)}, f32[256,128]{1,0:T(8,128)S(1)}, u32[]{:S(2)}, u32[]{:S(2)}) collective-permute-start(f32[256,128]{1,0:T(8,128)S(1)} %get-tuple-element.78), channel_id=1, source_target_pairs={{0,2},{1,3},{2,0},{3,1},{4,6},{5,7},{6,4},{7,5},{8,10},{9,11},{10,... | collective-permute-start | bytes 393224 | tf_op jit(solution)/shard_map/ppermute | solution.py:483
  40.3 10.6 %collective-permute-start.25 = (f32[256,128]{1,0:T(8,128)S(1)}, f32[256,128]{1,0:T(8,128)S(1)}, u32[]{:S(2)}, u32[]{:S(2)}) collective-permute-start(f32[256,128]{1,0:T(8,128)S(1)} %get-tuple-element.94), channel_id=1, source_target_pairs={{0,2},{1,3},{2,0},{3,1},{4,6},{5,7},{6,4},{7,5},{8,10},{9,11},{10,... | collective-permute-start | bytes 393224 | tf_op jit(solution)/shard_map/ppermute | solution.py:483
  41.7 7.2 %collective-permute-start.16 = (f32[256,128]{1,0:T(8,128)S(1)}, f32[256,128]{1,0:T(8,128)S(1)}, u32[]{:S(2)}, u32[]{:S(2)}) collective-permute-start(f32[256,128]{1,0:T(8,128)S(1)} %get-tuple-element.80), channel_id=1, source_target_pairs={{0,3},{1,2},{2,1},{3,0},{4,7},{5,6},{6,5},{7,4},{8,11},{9,10},{10,... | collective-permute-start | bytes 393224 | tf_op jit(solution)/shard_map/ppermute | solution.py:483
  41.8 10.5 %collective-permute-start.26 = (f32[256,128]{1,0:T(8,128)S(1)}, f32[256,128]{1,0:T(8,128)S(1)}, u32[]{:S(2)}, u32[]{:S(2)}) collective-permute-start(f32[256,128]{1,0:T(8,128)S(1)} %get-tuple-element.96), channel_id=1, source_target_pairs={{0,3},{1,2},{2,1},{3,0},{4,7},{5,6},{6,5},{7,4},{8,11},{9,10},{10,... | collective-permute-start | bytes 393224 | tf_op jit(solution)/shard_map/ppermute | solution.py:483
  44.2 9.0 %collective-permute-start.7 = (f32[128,128]{1,0:T(8,128)S(1)}, f32[128,128]{1,0:T(8,128)S(1)}, u32[]{:S(2)}, u32[]{:S(2)}) collective-permute-start(f32[128,128]{1,0:T(8,128)S(1)} %movers_message.3), channel_id=1, source_target_pairs={{0,4},{1,5},{2,6},{3,7},{4,8},{5,9},{6,10},{7,11},{8,12},{9,13},{1... | collective-permute-start | bytes 196616 | tf_op jit(solution)/shard_map/ppermute | solution.py:480
  48.9 25.3 %collective-permute-start.14 = (f32[896,128]{1,0:T(8,128)S(1)}, f32[896,128]{1,0:T(8,128)S(1)}, u32[]{:S(2)}, u32[]{:S(2)}) collective-permute-start(f32[896,128]{1,0:T(8,128)S(1)} %halo_message.4), channel_id=1, source_target_pairs={{0,4},{1,5},{2,6},{3,7},{4,8},{5,9},{6,10},{7,11},{8,12},{9,13},{1... | collective-permute-start | bytes 1376264 | tf_op jit(solution)/shard_map/ppermute | solution.py:480
  50.9 37.1 %collective-permute-start.24 = (f32[896,128]{1,0:T(8,128)S(1)}, f32[896,128]{1,0:T(8,128)S(1)}, u32[]{:S(2)}, u32[]{:S(2)}) collective-permute-start(f32[896,128]{1,0:T(8,128)S(1)} %halo_message.5), channel_id=1, source_target_pairs={{0,4},{1,5},{2,6},{3,7},{4,8},{5,9},{6,10},{7,11},{8,12},{9,13},{1... | collective-permute-start | bytes 1376264 | tf_op jit(solution)/shard_map/ppermute | solution.py:480
  52.3 21.8 %collective-permute-start.17 = (f32[128,128]{1,0:T(8,128)S(1)}, f32[128,128]{1,0:T(8,128)S(1)}, u32[]{:S(2)}, u32[]{:S(2)}) collective-permute-start(f32[128,128]{1,0:T(8,128)S(1)} %movers_message.4), channel_id=1, source_target_pairs={{0,4},{1,5},{2,6},{3,7},{4,8},{5,9},{6,10},{7,11},{8,12},{9,13},{1... | collective-permute-start | bytes 196616 | tf_op jit(solution)/shard_map/ppermute | solution.py:480
  53.2 34.8 %collective-permute-start.27 = (f32[128,128]{1,0:T(8,128)S(1)}, f32[128,128]{1,0:T(8,128)S(1)}, u32[]{:S(2)}, u32[]{:S(2)}) collective-permute-start(f32[128,128]{1,0:T(8,128)S(1)} %movers_message.5), channel_id=1, source_target_pairs={{0,4},{1,5},{2,6},{3,7},{4,8},{5,9},{6,10},{7,11},{8,12},{9,13},{1... | collective-permute-start | bytes 196616 | tf_op jit(solution)/shard_map/ppermute | solution.py:480
  68.0 34.9 %collective-permute-start.8 = (f32[960,128]{1,0:T(8,128)S(1)}, f32[960,128]{1,0:T(8,128)S(1)}, u32[]{:S(2)}, u32[]{:S(2)}) collective-permute-start(f32[960,128]{1,0:T(8,128)S(1)} %get-tuple-element.68), channel_id=1, source_target_pairs={{0,12},{1,13},{2,14},{3,15},{4,0},{5,1},{6,2},{7,3},{8,4},{9,5},{1... | collective-permute-start | bytes 1474568 | tf_op jit(solution)/shard_map/ppermute | solution.py:480
  87.8 19.6 %collective-permute-start.18 = (f32[960,128]{1,0:T(8,128)S(1)}, f32[960,128]{1,0:T(8,128)S(1)}, u32[]{:S(2)}, u32[]{:S(2)}) collective-permute-start(f32[960,128]{1,0:T(8,128)S(1)} %get-tuple-element.84), channel_id=1, source_target_pairs={{0,12},{1,13},{2,14},{3,15},{4,0},{5,1},{6,2},{7,3},{8,4},{9,5},{1... | collective-permute-start | bytes 1474568 | tf_op jit(solution)/shard_map/ppermute | solution.py:480
  101.5 11.6 %collective-permute-start.28 = (f32[960,128]{1,0:T(8,128)S(1)}, f32[960,128]{1,0:T(8,128)S(1)}, u32[]{:S(2)}, u32[]{:S(2)}) collective-permute-start(f32[960,128]{1,0:T(8,128)S(1)} %get-tuple-element.100), channel_id=1, source_target_pairs={{0,12},{1,13},{2,14},{3,15},{4,0},{5,1},{6,2},{7,3},{8,4},{9,5},{1... | collective-permute-start | bytes 1474568 | tf_op jit(solution)/shard_map/ppermute | solution.py:480
  103.9 10.2 %collective-permute-start.9 = (f32[384,128]{1,0:T(8,128)S(1)}, f32[384,128]{1,0:T(8,128)S(1)}, u32[]{:S(2)}, u32[]{:S(2)}) collective-permute-start(f32[384,128]{1,0:T(8,128)S(1)} %get-tuple-element.70), channel_id=1, source_target_pairs={{0,1},{1,0},{2,3},{3,2},{4,5},{5,4},{6,7},{7,6},{8,9},{9,8},{10,11... | collective-permute-start | bytes 589832 | tf_op jit(solution)/shard_map/ppermute | solution.py:483
  105.6 12.3 %collective-permute-start.10 = (f32[384,128]{1,0:T(8,128)S(1)}, f32[384,128]{1,0:T(8,128)S(1)}, u32[]{:S(2)}, u32[]{:S(2)}) collective-permute-start(f32[384,128]{1,0:T(8,128)S(1)} %get-tuple-element.71), channel_id=1, source_target_pairs={{0,2},{1,3},{2,0},{3,1},{4,6},{5,7},{6,4},{7,5},{8,10},{9,11},{10,... | collective-permute-start | bytes 589832 | tf_op jit(solution)/shard_map/ppermute | solution.py:483
  107.3 10.6 %collective-permute-start.11 = (f32[384,128]{1,0:T(8,128)S(1)}, f32[384,128]{1,0:T(8,128)S(1)}, u32[]{:S(2)}, u32[]{:S(2)}) collective-permute-start(f32[384,128]{1,0:T(8,128)S(1)} %get-tuple-element.72), channel_id=1, source_target_pairs={{0,3},{1,2},{2,1},{3,0},{4,7},{5,6},{6,5},{7,4},{8,11},{9,10},{10,... | collective-permute-start | bytes 589832 | tf_op jit(solution)/shard_map/ppermute | solution.py:483
  108.3 10.3 %collective-permute-start.19 = (f32[384,128]{1,0:T(8,128)S(1)}, f32[384,128]{1,0:T(8,128)S(1)}, u32[]{:S(2)}, u32[]{:S(2)}) collective-permute-start(f32[384,128]{1,0:T(8,128)S(1)} %get-tuple-element.86), channel_id=1, source_target_pairs={{0,1},{1,0},{2,3},{3,2},{4,5},{5,4},{6,7},{7,6},{8,9},{9,8},{10,11... | collective-permute-start | bytes 589832 | tf_op jit(solution)/shard_map/ppermute | solution.py:483
  113.1 6.9 %collective-permute-start.20 = (f32[384,128]{1,0:T(8,128)S(1)}, f32[384,128]{1,0:T(8,128)S(1)}, u32[]{:S(2)}, u32[]{:S(2)}) collective-permute-start(f32[384,128]{1,0:T(8,128)S(1)} %get-tuple-element.87), channel_id=1, source_target_pairs={{0,2},{1,3},{2,0},{3,1},{4,6},{5,7},{6,4},{7,5},{8,10},{9,11},{10,... | collective-permute-start | bytes 589832 | tf_op jit(solution)/shard_map/ppermute | solution.py:483
  114.1 12.5 %collective-permute-start.21 = (f32[384,128]{1,0:T(8,128)S(1)}, f32[384,128]{1,0:T(8,128)S(1)}, u32[]{:S(2)}, u32[]{:S(2)}) collective-permute-start(f32[384,128]{1,0:T(8,128)S(1)} %get-tuple-element.88), channel_id=1, source_target_pairs={{0,3},{1,2},{2,1},{3,0},{4,7},{5,6},{6,5},{7,4},{8,11},{9,10},{10,... | collective-permute-start | bytes 589832 | tf_op jit(solution)/shard_map/ppermute | solution.py:483
  117.9 8.7 %collective-permute-start.29 = (f32[384,128]{1,0:T(8,128)S(1)}, f32[384,128]{1,0:T(8,128)S(1)}, u32[]{:S(2)}, u32[]{:S(2)}) collective-permute-start(f32[384,128]{1,0:T(8,128)S(1)} %get-tuple-element.102), channel_id=1, source_target_pairs={{0,1},{1,0},{2,3},{3,2},{4,5},{5,4},{6,7},{7,6},{8,9},{9,8},{10,11... | collective-permute-start | bytes 589832 | tf_op jit(solution)/shard_map/ppermute | solution.py:483
  117.9 10.5 %collective-permute-start.30 = (f32[384,128]{1,0:T(8,128)S(1)}, f32[384,128]{1,0:T(8,128)S(1)}, u32[]{:S(2)}, u32[]{:S(2)}) collective-permute-start(f32[384,128]{1,0:T(8,128)S(1)} %get-tuple-element.103), channel_id=1, source_target_pairs={{0,2},{1,3},{2,0},{3,1},{4,6},{5,7},{6,4},{7,5},{8,10},{9,11},{10,... | collective-permute-start | bytes 589832 | tf_op jit(solution)/shard_map/ppermute | solution.py:483
  118.5 14.9 %collective-permute-start.31 = (f32[384,128]{1,0:T(8,128)S(1)}, f32[384,128]{1,0:T(8,128)S(1)}, u32[]{:S(2)}, u32[]{:S(2)}) collective-permute-start(f32[384,128]{1,0:T(8,128)S(1)} %get-tuple-element.104), channel_id=1, source_target_pairs={{0,3},{1,2},{2,1},{3,0},{4,7},{5,6},{6,5},{7,4},{8,11},{9,10},{10,... | collective-permute-start | bytes 589832 | tf_op jit(solution)/shard_map/ppermute | solution.py:483
where the time goes:
time: 136 us
  Pallas kernels  57.4 us (42%)
  starting transfers between devices  39.8 us (29%)
  waiting for transfers between devices  34.2 us (25%)
  local copies, waits for them, and re-layouts  3.79 us (3%)
    pallas_call x3, Pallas kernels, attend(): pl.pallas_call(functools.partial(attend_kernel, total, h), out_shape=[jax...  40.5 us
    ppermute x23, starting transfers between devices, swap(): return lax.ppermute(x, 'ctx', [(i, i ^ bit) for i in range(count)])  29.1 us
    ppermute x23, waiting for transfers between devices, swap(): return lax.ppermute(x, 'ctx', [(i, i ^ bit) for i in range(count)])  25.7 us
    ppermute x9, starting transfers between devices, along_z(): lax.ppermute(x, 'ctx', [(i, (i + step * PLANE) % count) for i in range(co...  10.7 us
    ppermute x9, waiting for transfers between devices, along_z(): lax.ppermute(x, 'ctx', [(i, (i + step * PLANE) % count) for i in range(co...  8.53 us
    pallas_call x2, Pallas kernels, pack_heads(): pl.pallas_call(functools.partial(pack_kernel, first_of, with_meta), out_s...  6.97 us
    unnamed x14, local copies, waits for them, and re-layouts  3.62 us
    pallas_call x3, Pallas kernels, finish(): pl.pallas_call(functools.partial(finish_kernel, total), out_shape=[jax.Sh...  2.81 us
  transfers between devices with their start and end apart: 32, of which 12 were waited for; matrix products, arithmetic and copies ran while one was open for 0% of the time, Pallas kernels for 38%

commit v1 on v0

v1 whole, which is shorter than its diff:
```python
import functools

import jax
import jax.numpy as jnp
from jax import lax
from jax.experimental import pallas as pl
from jax.experimental.pallas import tpu as pltpu
from jax.sharding import PartitionSpec as P

HEAD_DIM = 64
CELL = 64
CELLS = 4
ROWS = 256
PLANE = 4
HEADS = 3
HALO = 14
F32 = jnp.float32
BF16 = jnp.bfloat16
VMEM = pltpu.VMEM
NEGATIVE = -1e30
SCALE = HEAD_DIM ** -0.5


def vspec():
    return pl.BlockSpec(memory_space=pltpu.VMEM)


def sspec():
    return pl.BlockSpec(memory_space=pltpu.SMEM)


def params(limit=32):
    return pltpu.CompilerParams(vmem_limit_bytes=limit << 20)


def cost(flops, nbytes):
    return pl.CostEstimate(flops=flops, bytes_accessed=nbytes, transcendentals=0)


def lanes(shape):
    return lax.broadcasted_iota(jnp.int32, shape, 1)


def swap_half(x):
    return pltpu.roll(x, 64, 1)


def join(low, high):
    return jnp.where(lanes(low.shape) < 64, low, high)


def cells(i):
    return pl.ds(pl.multiple_of(i * CELL, CELL), CELL)


def head_blocks(info, c, s, a_ref, b_ref, grads):
    r = pl.ds(c * CELL, CELL)
    j = lax.bitwise_xor(info[24], s)
    first = pl.ds(pl.multiple_of(j * 128, 128), 128)
    last = pl.ds(pl.multiple_of((4 + j // 2) * 128, 128), 128)
    odd = (j % 2) == 1

    def load(lane_tile):
        a, b = a_ref[r, lane_tile], b_ref[r, lane_tile]
        if grads:
            row = lax.broadcasted_iota(jnp.int32, (CELL, 128), 0)
            a, b = a * SCALE, jnp.where(row < info[4 + c], b, 0.0)
        return a, b

    def zero():
        a, b = load(first)
        return join(a, swap_half(b))

    def one():
        a, b = load(first)
        return join(swap_half(a), b)

    def two():
        a, b = load(last)
        return join(jnp.where(odd, swap_half(a), a), jnp.where(odd, b, swap_half(b)))

    return zero, one, two


def pack_first_kernel(info, k_ref, v_ref, *outs):
    lane = lax.broadcasted_iota(jnp.int32, (8, 128), 1)
    meta = jnp.zeros((8, 128), F32)
    for i in range(20):
        meta = jnp.where(lane == i, info[i].astype(F32), meta)
    for s in range(PLANE):
        outs[s][pl.ds(ROWS, 8), :] = meta
        for c in range(CELLS):
            blocks = head_blocks(info, c, s, k_ref, v_ref, False)
            outs[s][pl.ds(c * CELL, CELL), :] = blocks[0]()


def pack_rest_kernel(info, k_ref, v_ref, q_ref, g_ref, *outs):
    mine, core, near, far = outs[0], outs[1], outs[2:5], outs[5:8]
    for s in range(PLANE):
        for c in range(CELLS):
            kv = head_blocks(info, c, s, k_ref, v_ref, False)
            qg = head_blocks(info, c, s, q_ref, g_ref, True)
            for i, block in enumerate((kv[1], kv[2], qg[0], qg[1], qg[2])):
                if s < 2:
                    outs[s][pl.ds(i * ROWS + c * CELL, CELL), :] = block()
                else:
                    part, row0 = ((1, 0), (2, 0), (0, 0), (1, ROWS), (2, ROWS))[i]
                    (near, far)[s - 2][part][pl.ds(row0 + c * CELL, CELL), :] = block()


def pack(kernel, shapes, name, info, *arrays):
    return pl.pallas_call(
        kernel,
        out_shape=[jax.ShapeDtypeStruct(s, F32) for s in shapes],
        in_specs=[sspec()] + [vspec()] * len(arrays),
        out_specs=[vspec()] * len(shapes),
        compiler_params=params(),
        cost_estimate=cost(1 << 20, 3 << 20),
        name=name,
    )(info, *arrays)


def walk(meta, start, total, visit):
    rank = jnp.int32(0)
    for s in range(PLANE):
        for c in range(CELLS):
            rel = lax.rem(meta[s, c] - start + total, total)
            moved = rel >= 16
            slot = jnp.where(moved, 12 + rank, rel - 4)
            visit(s, c, rel, slot)
            rank = rank + moved.astype(jnp.int32)


def halo_kernel(total, kv_rows, qg_rows, with_meta, info, meta, *refs):
    kv, qg, out = refs[:4], refs[4:-1], refs[-1]
    queries = 0 if kv_rows is None else HALO

    def visit(s, c, rel, slot):
        if kv_rows is not None:

            @pl.when(rel >= 4)
            def _():
                out[cells(slot), :] = kv[s][pl.ds(kv_rows[s] + c * CELL, CELL), :]

        if qg_rows is not None:

            @pl.when(rel >= 16)
            def _():
                out[cells(queries + slot - 12), :] = qg[s][pl.ds(qg_rows[s] + c * CELL, CELL), :]

    walk(meta, info[25], total, visit)
    if with_meta:
        out[pl.ds(HALO * CELL, 8), :] = jnp.zeros((8, 128), F32)
        for s in range(PLANE):
            out[pl.ds(HALO * CELL + s, 1), :] = kv[s][pl.ds(ROWS, 1), :]


def halo_message(total, info, meta, kv, qg, with_meta=False):
    rows, arrays = 0, []
    if kv is not None:
        rows += HALO * CELL
        arrays += [x for x, _ in kv]
    else:
        arrays += [x for x, _ in qg]
    if qg is not None:
        rows += 2 * CELL
        arrays += [x for x, _ in qg]
    rows += 8 if with_meta else 0
    firsts = [None if x is None else [r for _, r in x] for x in (kv, qg)]
    return pl.pallas_call(
        functools.partial(halo_kernel, total, *firsts, with_meta),
        out_shape=jax.ShapeDtypeStruct((rows, 128), F32),
        in_specs=[sspec()] * 2 + [vspec()] * len(arrays),
        out_specs=vspec(),
        compiler_params=params(),
        cost_estimate=cost(1 << 10, 1 << 20),
        name="halo_message",
    )(info, meta, *arrays)


def split(x):
    high = x.astype(BF16).astype(F32)
    return high, x - high


def nt(a, b):
    return lax.dot_general(a, b, (((1,), (1,)), ((), ())), preferred_element_type=F32)


def nn(a, b):
    return lax.dot_general(a, b, (((1,), (0,)), ((), ())), preferred_element_type=F32)


def tn(a, b):
    return lax.dot_general(a, b, (((0,), (0,)), ((), ())), preferred_element_type=F32)


def attend_kernel(total, kv_rows, qg_rows, m_row, info, meta, meta_prev, *refs):
    kv, halo, qg, qgm = refs[:4], refs[4], refs[5:9], refs[9]
    dkv, dq, back = refs[10:13]
    kcat, vcat, kt, acc_k, acc_v, qcat, gcat, qrhs, grhs, dq_scr = refs[13:23]
    pairs = (refs[23:25], refs[25:27])
    start = info[25]
    start_prev = info[26]
    lane = lax.broadcasted_iota(jnp.int32, (CELL, 128), 1)
    low = lane < 64
    lane16 = lax.broadcasted_iota(jnp.int32, (16, 128), 1)
    row16 = lax.broadcasted_iota(jnp.int32, (16, 128), 0)

    def put_key(x, slot, m, s, c):
        length = m[s, 4 + c]
        parts = []
        for i in range(4):
            limit = length - 16 * i
            if i > 0:
                limit = jnp.where(m[s, 7 + 3 * c + i] > 0, 0, limit)
            parts.append(jnp.where((row16 >= limit) & (lane16 == 64), NEGATIVE, 0.0))
        bias = jnp.concatenate(parts, axis=0)
        high, rest = split(x)
        high_r, rest_r = swap_half(high), swap_half(rest)
        mid, least = split(rest)
        kcat[cells(slot), pl.ds(0, 128)] = jnp.where(low, high, rest_r).astype(BF16)
        kcat[cells(slot), pl.ds(128, 128)] = jnp.where(low, high, bias).astype(BF16)
        kcat[cells(slot), pl.ds(256, 128)] = jnp.where(low, mid, swap_half(least)).astype(BF16)
        kcat[cells(slot), pl.ds(384, 128)] = jnp.where(low, high, 0.0).astype(BF16)
        vcat[cells(slot), pl.ds(0, 128)] = jnp.where(low, high_r, rest).astype(BF16)
        vcat[cells(slot), pl.ds(128, 128)] = jnp.where(low, high_r, 0.0).astype(BF16)

    one = jnp.where(lane == 64, 1.0, 0.0)

    def put_query(x, slot):
        high, rest = split(x)
        high_r, rest_r = swap_half(high), swap_half(rest)
        qcat[cells(slot), pl.ds(0, 128)] = jnp.where(low, high, high_r).astype(BF16)
        qcat[cells(slot), pl.ds(128, 128)] = jnp.where(low, rest, one).astype(BF16)
        mid, least = split(rest)
        qcat[cells(slot), pl.ds(256, 128)] = jnp.where(low, mid, high_r).astype(BF16)
        qcat[cells(slot), pl.ds(384, 128)] = jnp.where(low, least, 0.0).astype(BF16)
        gcat[cells(slot), pl.ds(0, 128)] = jnp.where(low, high_r, high).astype(BF16)
        gcat[cells(slot), pl.ds(128, 128)] = jnp.where(low, rest_r, 0.0).astype(BF16)
        qrhs[cells(slot), :] = jnp.where(low, high, rest_r).astype(BF16)
        grhs[cells(slot), :] = jnp.where(low, rest_r, high).astype(BF16)

    def own(s, c, rel, slot):
        here = rel < 16
        put_key(kv[s][pl.ds(kv_rows[s] + c * CELL, CELL), :], jnp.where(here, 12 + rel, 28), meta, s, c)
        put_query(qg[s][pl.ds(qg_rows[s] + c * CELL, CELL), :], jnp.where(here, rel, 16))

    walk(meta, start, total, own)
    came = [jnp.int32(0), jnp.int32(0)]

    def before(s, c, rel, slot):
        here = rel >= 4
        x = halo[cells(jnp.where(here, slot, 0)), :]
        put_key(x, jnp.where(here, rel - 4, 28), meta_prev, s, c)
        for i in range(2):
            came[i] = jnp.where((rel >= 16) & (slot == 12 + i), rel - 16, came[i])

    walk(meta_prev, start_prev, total, before)
    for i in range(2):
        put_query(qgm[pl.ds(m_row + i * CELL, CELL), :], came[i])
    for j in range(7):
        kt[:, pl.ds(j * ROWS, ROWS)] = kcat[pl.ds(j * ROWS, ROWS), pl.ds(0, 128)].T
    acc_k[...] = jnp.zeros(acc_k.shape, F32)
    acc_v[...] = jnp.zeros(acc_v.shape, F32)

    def fold(x, op):
        out = x[0:8]
        for i in range(1, x.shape[0] // 8):
            out = op(out, x[8 * i : 8 * i + 8])
        return out

    def block(b, carry):
        s_scr, d_scr = pairs[b % 2 if isinstance(b, int) else 0]

        def rows(i, n=ROWS):
            return pl.ds(i * ROWS if isinstance(i, int) else pl.multiple_of(i * ROWS, ROWS), n)

        q_rows = rows(b)
        top = None
        for c in range(4):
            scores = nt(kcat[rows(b + c), :], qcat[q_rows, :])
            s_scr[rows(c), :] = scores
            part = fold(scores, jnp.maximum)
            top = part if top is None else jnp.maximum(top, part)
        top = jnp.max(top, axis=0, keepdims=True)
        size = jnp.zeros((8, ROWS), F32)
        dots = jnp.zeros((8, ROWS), F32)
        for c in range(4):
            weights = jnp.exp(s_scr[rows(c), :] - top)
            grad_weights = nt(vcat[rows(b + c), :], gcat[q_rows, :])
            d_scr[rows(c), :] = grad_weights
            s_scr[rows(c), :] = weights
            size = size + fold(weights, jnp.add)
            dots = dots + fold(weights * grad_weights, jnp.add)
        inverse = 1.0 / jnp.sum(size, axis=0, keepdims=True)
        delta = jnp.sum(dots, axis=0, keepdims=True) * inverse
        dq_t = jnp.zeros((128, ROWS), F32)
        for c in range(4):
            weights = s_scr[rows(c), :] * inverse
            grad_scores = weights * (d_scr[rows(c), :] - delta)
            high = weights.astype(BF16)
            rest = (weights - high.astype(F32)).astype(BF16)
            acc_v[rows(b + c), :] += nn(high, grhs[q_rows, :]) + nn(rest, grhs[q_rows, :])
            high = grad_scores.astype(BF16)
            rest = (grad_scores - high.astype(F32)).astype(BF16)
            acc_k[rows(b + c), :] += nn(high, qrhs[q_rows, :]) + nn(rest, qrhs[q_rows, :])
            keys = kt[:, rows(b + c)]
            dq_t = dq_t + nn(keys, high) + nn(keys, rest)
        dq_t = (dq_t[0:64] + dq_t[64:128]) * SCALE
        dq_scr[q_rows, :] = jnp.concatenate([dq_t, dq_t], axis=0).T
        return carry

    for b in range(4):
        block(b, 0)

    def grad_kv(slot):
        a = acc_k[cells(slot), :]
        b = acc_v[cells(slot), :]
        return jnp.where(low, a + swap_half(a), b + swap_half(b))

    def own_out(s, c, rel, slot):
        here = rel < 16
        x = grad_kv(jnp.where(here, 12 + rel, 0))
        dkv[pl.ds(s * ROWS + c * CELL, CELL), :] = jnp.where(here, x, 0.0)
        x = dq_scr[cells(jnp.where(here, rel, 0)), :]
        half = pl.ds(s * 128 + (c // 2) * CELL, CELL)
        if c % 2 == 0:
            dq[half, :] = x
        else:
            dq[half, :] = jnp.where(low, dq[half, :], x)

    walk(meta, start, total, own_out)

    def before_out(s, c, rel, slot):
        here = rel >= 4
        back[cells(jnp.where(here, slot, HALO)), :] = grad_kv(jnp.where(here, rel - 4, 0))

    walk(meta_prev, start_prev, total, before_out)
    pair = jnp.where(low, dq_scr[cells(came[0]), :], dq_scr[cells(came[1]), :])
    back[pl.ds(HALO * CELL, CELL), :] = pair


def attend(total, info, meta, meta_prev, kv, halo, qg, qgm, m_row):
    kv_rows, qg_rows = ([r for _, r in x] for x in (kv, qg))
    kv, qg = ([x for x, _ in y] for y in (kv, qg))
    shapes = [(4 * ROWS, 128), (2 * ROWS, 128), (HALO * CELL + CELL, 128)]
    keys, queries = 29 * CELL, 17 * CELL
    return pl.pallas_call(
        functools.partial(attend_kernel, total, kv_rows, qg_rows, m_row),
        out_shape=[jax.ShapeDtypeStruct(s, F32) for s in shapes],
        in_specs=[sspec()] * 3 + [vspec()] * 10,
        out_specs=[vspec()] * 3,
        scratch_shapes=[
            VMEM((keys, 512), BF16),
            VMEM((keys, 256), BF16),
            VMEM((128, 28 * CELL), BF16),
            VMEM((28 * CELL, 128), F32),
            VMEM((28 * CELL, 128), F32),
            VMEM((queries, 512), BF16),
            VMEM((queries, 256), BF16),
            VMEM((queries, 128), BF16),
            VMEM((queries, 128), BF16),
            VMEM((queries, 128), F32),
        ]
        + [VMEM((4 * ROWS, ROWS), F32)] * 4,
        compiler_params=params(24),
        cost_estimate=cost(8 << 30, 8 << 20),
        name="attend",
    )(info, meta, meta_prev, *kv, halo, *qg, qgm)


OUT = ROWS + ROWS // 2


def finish_kernel(total, info, meta, dkv, dq, back, *outs):
    low = lanes((CELL, 128)) < 64
    pair = back[pl.ds(HALO * CELL, CELL), :]
    for s in range(PLANE):
        outs[s][pl.ds(ROWS, 128), :] = dq[pl.ds(s * 128, 128), :]

    def visit(s, c, rel, slot):
        out = outs[s]
        sent = rel >= 4
        x = jnp.where(sent, back[cells(jnp.where(sent, slot, 0)), :], 0.0)
        out[pl.ds(c * CELL, CELL), :] = dkv[pl.ds(s * ROWS + c * CELL, CELL), :] + x

        @pl.when(rel >= 16)
        def _():
            straight = (slot - 12) == (c % 2)
            x = jnp.where(straight, pair, swap_half(pair))
            half = pl.ds(ROWS + (c // 2) * CELL, CELL)
            out[half, :] = jnp.where(low == (c % 2 == 0), x, out[half, :])

    walk(meta, info[25], total, visit)


def finish(total, info, meta, dkv, dq, back):
    shapes = [(OUT, 128)] * 4
    return pl.pallas_call(
        functools.partial(finish_kernel, total),
        out_shape=[jax.ShapeDtypeStruct(s, F32) for s in shapes],
        in_specs=[sspec()] * 2 + [vspec()] * 3,
        out_specs=[vspec()] * 4,
        compiler_params=params(),
        cost_estimate=cost(1 << 10, 2 << 20),
        name="finish",
    )(info, meta, dkv, dq, back)


def unpack_kernel(info, *refs):
    parts, (oq, ok, ov) = refs[:12], refs[12:]
    me = info[24]

    def grads(s, c, h):
        return parts[4 * h + s][pl.ds(c * CELL, CELL), :]

    def query(s, c, h):
        x = parts[4 * h + s][pl.ds(ROWS + (c // 2) * CELL, CELL), :]
        return x, swap_half(x)

    for s in range(PLANE):
        j = lax.bitwise_xor(me, s)
        first = pl.ds(pl.multiple_of(j * 128, 128), 128)
        for c in range(CELLS):
            r = pl.ds(c * CELL, CELL)
            a, b = grads(s, c, 0), grads(s, c, 1)
            ok[r, first] = join(a, swap_half(b))
            ov[r, first] = join(swap_half(a), b)
            x0, y0 = query(s, c, 0)
            x1, y1 = query(s, c, 1)
            oq[r, first] = join(x0, y1) if c % 2 == 0 else join(y0, x1)
    for s in (0, 2):
        j = lax.bitwise_xor(me, s)
        even = (j % 2) == 0
        last = pl.ds(pl.multiple_of((4 + j // 2) * 128, 128), 128)
        for c in range(CELLS):
            r = pl.ds(c * CELL, CELL)
            u, w = grads(s, c, 2), grads(s + 1, c, 2)
            a, b = jnp.where(even, u, w), jnp.where(even, w, u)
            ok[r, last] = join(a, swap_half(b))
            ov[r, last] = join(swap_half(a), b)
            u, w = query(s, c, 2)[0], query(s + 1, c, 2)[0]
            a, b = jnp.where(even, u, w), jnp.where(even, w, u)
            oq[r, last] = join(a, swap_half(b)) if c % 2 == 0 else join(swap_half(a), b)


def unpack_heads(info, parts, features):
    return pl.pallas_call(
        unpack_kernel,
        out_shape=[jax.ShapeDtypeStruct((ROWS, features), F32)] * 3,
        in_specs=[sspec()] + [vspec()] * 12,
        out_specs=[vspec()] * 3,
        compiler_params=params(),
        cost_estimate=cost(1 << 20, 5 << 20),
        name="unpack_heads",
    )(info, *[x for part in parts for x in part])


def after(x, *earlier):
    return lax.optimization_barrier((x, *earlier))[0]


def on_device(query_rows, key_rows, value_rows, grad_rows, placement, cell_lengths, gene_mask):
    count = lax.axis_size("ctx")
    total = count * CELLS
    index = lax.axis_index("ctx").astype(jnp.int32)
    plane = index // PLANE

    def along_z(x, step):
        return lax.ppermute(x, "ctx", [(i, (i + step * PLANE) % count) for i in range(count)])

    def swap(x, bit):
        return lax.ppermute(x, "ctx", [(i, i ^ bit) for i in range(count)])

    start = plane * (PLANE * CELLS)
    start_prev = lax.rem(start - PLANE * CELLS + total, total)
    tail = jnp.stack([jnp.int32(0)] * 4 + [index % PLANE, start, start_prev, jnp.int32(0)])
    info = jnp.concatenate([placement, cell_lengths, gene_mask.reshape(-1), tail])

    own0, core0, near0, far0 = pack(
        pack_first_kernel, [(ROWS + 8, 128)] * 4, "pack_first", info, key_rows, value_rows
    )
    near0, far0, core0 = swap(near0, 2), swap(far0, 3), swap(core0, 1)
    sizes = [5 * ROWS] * 2 + [ROWS, 2 * ROWS, 2 * ROWS] * 2
    own, core, *rest = pack(
        pack_rest_kernel,
        [(n, 128) for n in sizes],
        "pack_rest",
        after(info, own0),
        key_rows,
        value_rows,
        query_rows,
        grad_rows,
    )
    near, far = rest[:3], rest[3:]

    def across(i, *earlier):
        pair = (near[i], far[i])
        if earlier:
            pair = after(pair, *earlier)
        near[i], far[i] = swap(pair[0], 2), swap(pair[1], 3)

    across(0)
    first = after((core0, near0, far0), own)
    kv0 = [(x, 0) for x in (own0, *first)]
    meta = jnp.stack([x[ROWS, :32] for x, _ in kv0]).astype(jnp.int32)
    message0 = halo_message(total, info, meta, kv0, None, True)
    halo0 = along_z(message0, 1)
    core = swap(after(core, *first), 1)
    across(1, message0)

    def sources(row0, i, row1):
        return [(own, row0), (core, row0), (near[i], row1), (far[i], row1)]

    qg0 = sources(2 * ROWS, 0, 0)
    movers0 = halo_message(total, info, meta, None, qg0)
    qgm0 = along_z(movers0, 1)
    across(2, movers0)
    kv = [kv0, sources(0, 1, 0), sources(ROWS, 2, 0)]
    qg = [qg0, sources(3 * ROWS, 1, ROWS), sources(4 * ROWS, 2, ROWS)]
    messages = [message0] + [halo_message(total, info, meta, kv[h], qg[h]) for h in (1, 2)]
    halo = [halo0] + [along_z(messages[h], 1) for h in (1, 2)]
    movers = [(qgm0, 0), (halo[1], HALO * CELL), (halo[2], HALO * CELL)]
    meta_prev = halo0[HALO * CELL : HALO * CELL + 4, :32].astype(jnp.int32)

    parts = []
    turn = ()
    for h in range(HEADS):
        came, m_row = movers[h]
        sent = messages[h + 1 :][:1]
        info_h = after(info, *turn, *sent)
        dkv, dq, back = attend(total, info_h, meta, meta_prev, kv[h], halo[h], qg[h], came, m_row)
        turn = (dq,)
        mine, *outs = finish(total, info, meta, dkv, dq, along_z(back, -1))
        parts.append([mine] + [swap(x, i + 1) for i, x in enumerate(outs)])
    return tuple(unpack_heads(info, parts, query_rows.shape[1]))


def solution(mesh):
    rows = P(("groups", "ctx"), None)
    flat = P(("groups", "ctx"))
    return jax.shard_map(
        on_device,
        mesh=mesh,
        in_specs=(rows, rows, rows, rows, flat, flat, rows),
        out_specs=(rows, rows, rows),
        check_vma=False,
    )
```

time: 136 us -> 121 us (0.89)
  Pallas kernels: 57.4 us -> 39.1 us
  waiting for transfers between devices: 34.2 us -> 43.3 us
  starting transfers between devices: 39.8 us -> 33.4 us
    pallas_call x11 -> x9, Pallas kernels: 52 us -> 33.7 us  [the longest x3 28.1 us: attend(): pl.pallas_call(functools.partial(attend_kernel, total, kv_rows, qg_rows,...]
    ppermute x23 -> x19, starting transfers between devices: 29.1 us -> 20 us  [swap(): return lax.ppermute(x, 'ctx', [(i, i ^ bit) for i in range(count)])]
    ppermute x9 -> x7, waiting for transfers between devices: 8.53 us -> 15.5 us  [along_z(): lax.ppermute(x, 'ctx', [(i, (i + step * PLANE) % count) for i in range(co...]
    ppermute x9 -> x7, starting transfers between devices: 10.7 us -> 13.4 us  [along_z(): lax.ppermute(x, 'ctx', [(i, (i + step * PLANE) % count) for i in range(co...]
    ppermute x23 -> x19, waiting for transfers between devices: 25.7 us -> 27.8 us  [swap(): return lax.ppermute(x, 'ctx', [(i, i ^ bit) for i in range(count)])]
  transfers between devices with their start and end apart: 32 -> 26, of which waited for: 12 -> 13; matrix products, arithmetic and copies ran while one was open for 0% -> 0% of each run, Pallas kernels for 38% -> 30%
where the time goes in v1:
time: 121 us; the launch traced here: 120 us
  waiting for transfers between devices  43.3 us (36%)
  Pallas kernels  39.1 us (32%)
  starting transfers between devices  33.4 us (28%)
  local copies, waits for them, and re-layouts  3.79 us (3%)
    pallas_call x3, Pallas kernels, attend(): pl.pallas_call(functools.partial(attend_kernel, total, kv_rows, qg_rows,...  28.1 us
    ppermute x19, waiting for transfers between devices, swap(): return lax.ppermute(x, 'ctx', [(i, i ^ bit) for i in range(count)])  27.8 us
    ppermute x19, starting transfers between devices, swap(): return lax.ppermute(x, 'ctx', [(i, i ^ bit) for i in range(count)])  20 us
    ppermute x7, waiting for transfers between devices, along_z(): lax.ppermute(x, 'ctx', [(i, (i + step * PLANE) % count) for i in range(co...  15.5 us
    ppermute x7, starting transfers between devices, along_z(): lax.ppermute(x, 'ctx', [(i, (i + step * PLANE) % count) for i in range(co...  13.4 us
    unnamed x14, local copies, waits for them, and re-layouts  3.62 us
    pallas_call x4, Pallas kernels, halo_message(): pl.pallas_call(functools.partial(halo_kernel, total, *firsts, with_meta),...  3.22 us
    pallas_call x3, Pallas kernels, finish(): pl.pallas_call(functools.partial(finish_kernel, total), out_shape=[jax.Sh...  2.83 us
  transfers between devices with their start and end apart: 26, of which 13 were waited for; matrix products, arithmetic and copies ran while one was open for 0% of the time, Pallas kernels for 30%

profile of v1, /device:TPU:1, one launch (start us, length us, event | category | flops | bytes accessed | tf_op | source)
XLA Modules:
  0.0 120.4 jit_solution(15709157123746461009)
XLA Ops:
  0.7 0.7 copy-done.4
  1.3 0.1 reshape.9
  1.4 0.7 copy-done.5
  2.1 0.0 copy-done.6
  2.1 0.1 concatenate.3.info
  2.2 1.1 copy-done
  3.3 1.1 copy-done.1
  4.4 0.8 pack_first.1
  5.2 0.1 collective-permute-start
  5.3 2.7 %collective-permute-start.1 = (f32[264,128]{1,0:T(8,128)S(1)}, f32[264,128]{1,0:T(8,128)S(1)}, u32[]{:S(2)}, u32[]{:S(2)}) collective-permute-start(f32[264,128]{1,0:T(8,128)S(1)} %get-tuple-element.50), channel_id=1, source_target_pairs={{0,2},{1,3},{2,0},{3,1},{4,6},{5,7},{6,4},{7,5},{8,10},{9,11},{10,... | collective-permute-start | bytes 405512 | tf_op jit(solution)/shard_map/ppermute | solution.py:474
  8.0 0.0 collective-permute-start.2
  8.1 1.6 %pack_rest.1 = (f32[1280,128]{1,0:T(8,128)S(1)}, f32[1280,128]{1,0:T(8,128)S(1)}, f32[256,128]{1,0:T(8,128)S(1)}, f32[512,128]{1,0:T(8,128)S(1)}, f32[512,128]{1...) custom-call(s32[28]{0:T(128)S(1)} %concatenate.3.info, ...), custom_call_target="tpu_custom_call" | custom-call | flops 1048576 | bytes 3145728 | tf_op jit(solution)/shard_map/pack_rest/pallas_call | solution.py:112
  9.7 0.0 collective-permute-done.refs_1_
  9.7 2.2 %collective-permute-done.1.refs_2_ = f32[264,128]{1,0:T(8,128)S(1)} collective-permute-done((f32[264,128]{1,0:T(8,128)S(1)}, f32[264,128]{1,0:T(8,128)S(1)}, u32[]{:S(2)}, u32[]{:S(2)}) %collective-permute-start.1) | collective-permute-done | bytes 135200 | tf_op jit(solution)/shard_map/ppermute | solution.py:474
  11.9 2.9 %collective-permute-done.2.refs_3_ = f32[264,128]{1,0:T(8,128)S(1)} collective-permute-done((f32[264,128]{1,0:T(8,128)S(1)}, f32[264,128]{1,0:T(8,128)S(1)}, u32[]{:S(2)}, u32[]{:S(2)}) %collective-permute-start.2) | collective-permute-done | bytes 135200 | tf_op jit(solution)/shard_map/ppermute | solution.py:474
  14.8 0.4 collective-permute-start.3
  15.2 0.8 halo_message.4
  16.0 1.4 %collective-permute-start.6 = (f32[904,128]{1,0:T(8,128)S(1)}, f32[904,128]{1,0:T(8,128)S(1)}, u32[]{:S(2)}, u32[]{:S(2)}) collective-permute-start(f32[904,128]{1,0:T(8,128)S(1)} %halo_message.4), channel_id=1, source_target_pairs={{0,4},{1,5},{2,6},{3,7},{4,8},{5,9},{6,10},{7,11},{8,12},{9,13},{1... | collective-permute-start | bytes 1388552 | tf_op jit(solution)/shard_map/ppermute | solution.py:471
  17.4 1.2 %collective-permute-start.7 = (f32[256,128]{1,0:T(8,128)S(1)}, f32[256,128]{1,0:T(8,128)S(1)}, u32[]{:S(2)}, u32[]{:S(2)}) collective-permute-start(f32[256,128]{1,0:T(8,128)S(1)} %get-tuple-element.64), channel_id=1, source_target_pairs={{0,2},{1,3},{2,0},{3,1},{4,6},{5,7},{6,4},{7,5},{8,10},{9,11},{10,... | collective-permute-start | bytes 393224 | tf_op jit(solution)/shard_map/ppermute | solution.py:474
  18.6 0.9 collective-permute-start.8
  19.6 1.2 %collective-permute-start.4 = (f32[512,128]{1,0:T(8,128)S(1)}, f32[512,128]{1,0:T(8,128)S(1)}, u32[]{:S(2)}, u32[]{:S(2)}) collective-permute-start(f32[512,128]{1,0:T(8,128)S(1)} %get-tuple-element.61), channel_id=1, source_target_pairs={{0,2},{1,3},{2,0},{3,1},{4,6},{5,7},{6,4},{7,5},{8,10},{9,11},{10,... | collective-permute-start | bytes 786440 | tf_op jit(solution)/shard_map/ppermute | solution.py:474
  20.8 1.1 collective-permute-done.7.refs_2_.refs_6_.refs_7_
  21.9 3.6 %collective-permute-start.5 = (f32[512,128]{1,0:T(8,128)S(1)}, f32[512,128]{1,0:T(8,128)S(1)}, u32[]{:S(2)}, u32[]{:S(2)}) collective-permute-start(f32[512,128]{1,0:T(8,128)S(1)} %get-tuple-element.62), channel_id=1, source_target_pairs={{0,3},{1,2},{2,1},{3,0},{4,7},{5,6},{6,5},{7,4},{8,11},{9,10},{10,... | collective-permute-start | bytes 786440 | tf_op jit(solution)/shard_map/ppermute | solution.py:474
  25.4 1.1 collective-permute-done.8.refs_3_.refs_7_.refs_8_
  26.6 0.0 collective-permute-done.3.refs_1_.refs_5_.refs_6_
  26.6 0.8 halo_message.6
  27.3 1.3 %collective-permute-start.9 = (f32[128,128]{1,0:T(8,128)S(1)}, f32[128,128]{1,0:T(8,128)S(1)}, u32[]{:S(2)}, u32[]{:S(2)}) collective-permute-start(f32[128,128]{1,0:T(8,128)S(1)} %halo_message.6), channel_id=1, source_target_pairs={{0,4},{1,5},{2,6},{3,7},{4,8},{5,9},{6,10},{7,11},{8,12},{9,13},{1... | collective-permute-start | bytes 196616 | tf_op jit(solution)/shard_map/ppermute | solution.py:471
  28.7 1.5 %collective-permute-done.6.refs_4_ = f32[904,128]{1,0:T(8,128)S(1)} collective-permute-done((f32[904,128]{1,0:T(8,128)S(1)}, f32[904,128]{1,0:T(8,128)S(1)}, u32[]{:S(2)}, u32[]{:S(2)}) %collective-permute-start.6) | collective-permute-done | bytes 462880 | tf_op jit(solution)/shard_map/ppermute | solution.py:471
  30.2 0.3 collective-permute-done.4.refs_2_.refs_6_.refs_7_
  30.5 6.2 %collective-permute-done.5.refs_3_.refs_7_.refs_8_ = f32[512,128]{1,0:T(8,128)S(1)} collective-permute-done((f32[512,128]{1,0:T(8,128)S(1)}, f32[512,128]{1,0:T(8,128)S(1)}, u32[]{:S(2)}, u32[]{:S(2)}) %collective-permute-start.5) | collective-permute-done | bytes 262176 | tf_op jit(solution)/shard_map/ppermute | solution.py:474
  36.7 0.8 halo_message.5
  37.5 1.3 %collective-permute-start.16 = (f32[1024,128]{1,0:T(8,128)S(1)}, f32[1024,128]{1,0:T(8,128)S(1)}, u32[]{:S(2)}, u32[]{:S(2)}) collective-permute-start(f32[1024,128]{1,0:T(8,128)S(1)} %halo_message.5), channel_id=1, source_target_pairs={{0,4},{1,5},{2,6},{3,7},{4,8},{5,9},{6,10},{7,11},{8,12},{9,13},{1... | collective-permute-start | bytes 1572872 | tf_op jit(solution)/shard_map/ppermute | solution.py:471
  38.9 1.2 %collective-permute-start.14 = (f32[512,128]{1,0:T(8,128)S(1)}, f32[512,128]{1,0:T(8,128)S(1)}, u32[]{:S(2)}, u32[]{:S(2)}) collective-permute-start(f32[512,128]{1,0:T(8,128)S(1)} %get-tuple-element.75), channel_id=1, source_target_pairs={{0,2},{1,3},{2,0},{3,1},{4,6},{5,7},{6,4},{7,5},{8,10},{9,11},{10,... | collective-permute-start | bytes 786440 | tf_op jit(solution)/shard_map/ppermute | solution.py:474
  40.1 0.5 collective-permute-start.15
  40.6 9.4 %attend.3 = (f32[1024,128]{1,0:T(8,128)S(1)}, f32[512,128]{1,0:T(8,128)S(1)}, f32[960,128]{1,0:T(8,128)S(1)}) custom-call(s32[28]{0:T(128)S(1)} %concatenate.3.info, s32[4,32]{1,0:T(4,128)S(1)} %maximum_convert_fusion.meta, s32[4,32]{1,0:T(4,128)S(1)} %slice_convert_fusion.meta_prev, f32[264,128]{1,0:T(8,128)S(1)} %get-tuple-element.48.refs_0_, ...), custom_call_target="tpu_custom_call" | custom-call | flops 8589934592 | bytes 8388608 | tf_op jit(solution)/shard_map/attend/pallas_call | solution.py:349
  50.0 2.2 %collective-permute-start.10 = (f32[960,128]{1,0:T(8,128)S(1)}, f32[960,128]{1,0:T(8,128)S(1)}, u32[]{:S(2)}, u32[]{:S(2)}) collective-permute-start(f32[960,128]{1,0:T(8,128)S(1)} %get-tuple-element.68), channel_id=1, source_target_pairs={{0,12},{1,13},{2,14},{3,15},{4,0},{5,1},{6,2},{7,3},{8,4},{9,5},{1... | collective-permute-start | bytes 1474568 | tf_op jit(solution)/shard_map/ppermute | solution.py:471
  52.2 0.0 collective-permute-done.14.refs_2_.refs_6_.refs_7_
  52.2 0.7 collective-permute-done.15.refs_3_.refs_7_.refs_8_
  52.8 0.8 halo_message.7
  53.7 1.1 collective-permute-start.21
  54.7 9.4 %attend.4 = (f32[1024,128]{1,0:T(8,128)S(1)}, f32[512,128]{1,0:T(8,128)S(1)}, f32[960,128]{1,0:T(8,128)S(1)}) custom-call(s32[28]{0:T(128)S(1)} %concatenate.3.info, s32[4,32]{1,0:T(4,128)S(1)} %maximum_convert_fusion.meta, s32[4,32]{1,0:T(4,128)S(1)} %slice_convert_fusion.meta_prev, f32[1280,128]{1,0:T(8,128)S(1)} %get-tuple-element.53.refs_0_.refs_4_.refs_5_, ...), custom_call_target="tpu_custom_call" | custom-call | flops 8589934592 | bytes 8388608 | tf_op jit(solution)/shard_map/attend/pallas_call | solution.py:349
  64.1 2.5 %collective-permute-start.17 = (f32[960,128]{1,0:T(8,128)S(1)}, f32[960,128]{1,0:T(8,128)S(1)}, u32[]{:S(2)}, u32[]{:S(2)}) collective-permute-start(f32[960,128]{1,0:T(8,128)S(1)} %get-tuple-element.80), channel_id=1, source_target_pairs={{0,12},{1,13},{2,14},{3,15},{4,0},{5,1},{6,2},{7,3},{8,4},{9,5},{1... | collective-permute-start | bytes 1474568 | tf_op jit(solution)/shard_map/ppermute | solution.py:471
  66.6 8.7 %collective-permute-done.21.refs_4_.refs_9_ = f32[1024,128]{1,0:T(8,128)S(1)} collective-permute-done((f32[1024,128]{1,0:T(8,128)S(1)}, f32[1024,128]{1,0:T(8,128)S(1)}, u32[]{:S(2)}, u32[]{:S(2)}) %collective-permute-start.21) | collective-permute-done | bytes 524320 | tf_op jit(solution)/shard_map/ppermute | solution.py:471
  75.3 9.4 %attend.5 = (f32[1024,128]{1,0:T(8,128)S(1)}, f32[512,128]{1,0:T(8,128)S(1)}, f32[960,128]{1,0:T(8,128)S(1)}) custom-call(s32[28]{0:T(128)S(1)} %concatenate.3.info, s32[4,32]{1,0:T(4,128)S(1)} %maximum_convert_fusion.meta, s32[4,32]{1,0:T(4,128)S(1)} %slice_convert_fusion.meta_prev, f32[1280,128]{1,0:T(8,128)S(1)} %get-tuple-element.53.refs_0_.refs_4_.refs_5_, ...), custom_call_target="tpu_custom_call" | custom-call | flops 8589934592 | bytes 8388608 | tf_op jit(solution)/shard_map/attend/pallas_call | solution.py:349
  84.7 3.5 %collective-permute-start.22 = (f32[960,128]{1,0:T(8,128)S(1)}, f32[960,128]{1,0:T(8,128)S(1)}, u32[]{:S(2)}, u32[]{:S(2)}) collective-permute-start(f32[960,128]{1,0:T(8,128)S(1)} %get-tuple-element.88), channel_id=1, source_target_pairs={{0,12},{1,13},{2,14},{3,15},{4,0},{5,1},{6,2},{7,3},{8,4},{9,5},{1... | collective-permute-start | bytes 1474568 | tf_op jit(solution)/shard_map/ppermute | solution.py:471
  88.3 0.9 finish.3
  89.2 0.9 collective-permute-start.11
  90.1 1.2 %collective-permute-start.12 = (f32[384,128]{1,0:T(8,128)S(1)}, f32[384,128]{1,0:T(8,128)S(1)}, u32[]{:S(2)}, u32[]{:S(2)}) collective-permute-start(f32[384,128]{1,0:T(8,128)S(1)} %get-tuple-element.71), channel_id=1, source_target_pairs={{0,2},{1,3},{2,0},{3,1},{4,6},{5,7},{6,4},{7,5},{8,10},{9,11},{10,... | collective-permute-start | bytes 589832 | tf_op jit(solution)/shard_map/ppermute | solution.py:474
  91.3 0.5 collective-permute-start.13
  91.8 0.0 collective-permute-done.17.back
  91.8 0.9 finish.4
  92.8 0.2 collective-permute-start.18
  93.0 5.3 %collective-permute-done.22.back = f32[960,128]{1,0:T(8,128)S(1)} collective-permute-done((f32[960,128]{1,0:T(8,128)S(1)}, f32[960,128]{1,0:T(8,128)S(1)}, u32[]{:S(2)}, u32[]{:S(2)}) %collective-permute-start.22) | collective-permute-done | bytes 491552 | tf_op jit(solution)/shard_map/ppermute | solution.py:471
  98.3 1.2 collective-permute-start.19
  99.5 0.9 finish.5
  100.5 1.9 %collective-permute-start.20 = (f32[384,128]{1,0:T(8,128)S(1)}, f32[384,128]{1,0:T(8,128)S(1)}, u32[]{:S(2)}, u32[]{:S(2)}) collective-permute-start(f32[384,128]{1,0:T(8,128)S(1)} %get-tuple-element.84), channel_id=1, source_target_pairs={{0,3},{1,2},{2,1},{3,0},{4,7},{5,6},{6,5},{7,4},{8,11},{9,10},{10,... | collective-permute-start | bytes 589832 | tf_op jit(solution)/shard_map/ppermute | solution.py:474
  102.4 0.0 collective-permute-done.12.refs_2_
  102.4 0.0 collective-permute-start.23
  102.4 1.3 %collective-permute-start.24 = (f32[384,128]{1,0:T(8,128)S(1)}, f32[384,128]{1,0:T(8,128)S(1)}, u32[]{:S(2)}, u32[]{:S(2)}) collective-permute-start(f32[384,128]{1,0:T(8,128)S(1)} %get-tuple-element.91), channel_id=1, source_target_pairs={{0,2},{1,3},{2,0},{3,1},{4,6},{5,7},{6,4},{7,5},{8,10},{9,11},{10,... | collective-permute-start | bytes 589832 | tf_op jit(solution)/shard_map/ppermute | solution.py:474
  103.6 0.9 collective-permute-start.25
  104.5 5.5 %collective-permute-done.20.refs_7_ = f32[384,128]{1,0:T(8,128)S(1)} collective-permute-done((f32[384,128]{1,0:T(8,128)S(1)}, f32[384,128]{1,0:T(8,128)S(1)}, u32[]{:S(2)}, u32[]{:S(2)}) %collective-permute-start.20) | collective-permute-done | bytes 196640 | tf_op jit(solution)/shard_map/ppermute | solution.py:474
  110.0 3.3 %collective-permute-done.24.refs_10_ = f32[384,128]{1,0:T(8,128)S(1)} collective-permute-done((f32[384,128]{1,0:T(8,128)S(1)}, f32[384,128]{1,0:T(8,128)S(1)}, u32[]{:S(2)}, u32[]{:S(2)}) %collective-permute-start.24) | collective-permute-done | bytes 196640 | tf_op jit(solution)/shard_map/ppermute | solution.py:474
  113.3 4.5 %collective-permute-done.25.refs_11_ = f32[384,128]{1,0:T(8,128)S(1)} collective-permute-done((f32[384,128]{1,0:T(8,128)S(1)}, f32[384,128]{1,0:T(8,128)S(1)}, u32[]{:S(2)}, u32[]{:S(2)}) %collective-permute-start.25) | collective-permute-done | bytes 196640 | tf_op jit(solution)/shard_map/ppermute | solution.py:474
  117.8 2.6 %unpack_heads.1 = (f32[256,768]{1,0:T(8,128)}, f32[256,768]{1,0:T(8,128)}, f32[256,768]{1,0:T(8,128)}) custom-call(s32[28]{0:T(128)S(1)} %concatenate.3.info, f32[384,128]{1,0:T(8,128)S(1)} %get-tuple-element.69.refs_0_, f32[384,128]{1,0:T(8,128)S(1)} %collective-permute-done.11.refs_1_, f32[384,128]{1,0:T(8,128)S(1)} %collective-permute-done.12.refs_2_, ...), custom_call_target="tpu_custom_call" | custom-call | flops 1048576 | bytes 5242880 | tf_op jit(solution)/shard_map/unpack_heads/pallas_call | solution.py:449
  (24 shorter events, 0.1 us)
Async XLA Ops:
  0.7 0.7 copy-start.4
  1.4 0.7 copy-start.5
  1.4 0.7 copy-start.6
  2.2 1.1 copy-start
  3.3 1.1 copy-start.1
  4.4 3.6 %copy-start.2 = (f32[256,768]{1,0:T(8,128)S(1)}, f32[256,768]{1,0:T(8,128)}, u32[]{:S(2)}) copy-start(f32[256,768]{1,0:T(8,128)} %q_ref.1) | copy-start | bytes 2359300
  4.4 3.6 %copy-start.3 = (f32[256,768]{1,0:T(8,128)S(1)}, f32[256,768]{1,0:T(8,128)}, u32[]{:S(2)}) copy-start(f32[256,768]{1,0:T(8,128)} %g_ref.1) | copy-start | bytes 2359300
  5.2 4.5 %collective-permute-start = (f32[264,128]{1,0:T(8,128)S(1)}, f32[264,128]{1,0:T(8,128)S(1)}, u32[]{:S(2)}, u32[]{:S(2)}) collective-permute-start(f32[264,128]{1,0:T(8,128)S(1)} %get-tuple-element.49), channel_id=1, source_target_pairs={{0,1},{1,0},{2,3},{3,2},{4,5},{5,4},{6,7},{7,6},{8,9},{9,8},{10,11... | collective-permute-start | bytes 405512 | tf_op jit(solution)/shard_map/ppermute | solution.py:474
  5.3 6.6 %collective-permute-start.1 = (f32[264,128]{1,0:T(8,128)S(1)}, f32[264,128]{1,0:T(8,128)S(1)}, u32[]{:S(2)}, u32[]{:S(2)}) collective-permute-start(f32[264,128]{1,0:T(8,128)S(1)} %get-tuple-element.50), channel_id=1, source_target_pairs={{0,2},{1,3},{2,0},{3,1},{4,6},{5,7},{6,4},{7,5},{8,10},{9,11},{10,... | collective-permute-start | bytes 405512 | tf_op jit(solution)/shard_map/ppermute | solution.py:474
  8.0 6.8 %collective-permute-start.2 = (f32[264,128]{1,0:T(8,128)S(1)}, f32[264,128]{1,0:T(8,128)S(1)}, u32[]{:S(2)}, u32[]{:S(2)}) collective-permute-start(f32[264,128]{1,0:T(8,128)S(1)} %get-tuple-element.51), channel_id=1, source_target_pairs={{0,3},{1,2},{2,1},{3,0},{4,7},{5,6},{6,5},{7,4},{8,11},{9,10},{10,... | collective-permute-start | bytes 405512 | tf_op jit(solution)/shard_map/ppermute | solution.py:474
  14.8 11.8 %collective-permute-start.3 = (f32[1280,128]{1,0:T(8,128)S(1)}, f32[1280,128]{1,0:T(8,128)S(1)}, u32[]{:S(2)}, u32[]{:S(2)}) collective-permute-start(f32[1280,128]{1,0:T(8,128)S(1)} %get-tuple-element.58), channel_id=1, source_target_pairs={{0,1},{1,0},{2,3},{3,2},{4,5},{5,4},{6,7},{7,6},{8,9},{9,8},{10,11... | collective-permute-start | bytes 1966088 | tf_op jit(solution)/shard_map/ppermute | solution.py:474
  16.0 14.2 %collective-permute-start.6 = (f32[904,128]{1,0:T(8,128)S(1)}, f32[904,128]{1,0:T(8,128)S(1)}, u32[]{:S(2)}, u32[]{:S(2)}) collective-permute-start(f32[904,128]{1,0:T(8,128)S(1)} %halo_message.4), channel_id=1, source_target_pairs={{0,4},{1,5},{2,6},{3,7},{4,8},{5,9},{6,10},{7,11},{8,12},{9,13},{1... | collective-permute-start | bytes 1388552 | tf_op jit(solution)/shard_map/ppermute | solution.py:471
  17.4 4.5 %collective-permute-start.7 = (f32[256,128]{1,0:T(8,128)S(1)}, f32[256,128]{1,0:T(8,128)S(1)}, u32[]{:S(2)}, u32[]{:S(2)}) collective-permute-start(f32[256,128]{1,0:T(8,128)S(1)} %get-tuple-element.64), channel_id=1, source_target_pairs={{0,2},{1,3},{2,0},{3,1},{4,6},{5,7},{6,4},{7,5},{8,10},{9,11},{10,... | collective-permute-start | bytes 393224 | tf_op jit(solution)/shard_map/ppermute | solution.py:474
  18.6 7.9 %collective-permute-start.8 = (f32[256,128]{1,0:T(8,128)S(1)}, f32[256,128]{1,0:T(8,128)S(1)}, u32[]{:S(2)}, u32[]{:S(2)}) collective-permute-start(f32[256,128]{1,0:T(8,128)S(1)} %get-tuple-element.65), channel_id=1, source_target_pairs={{0,3},{1,2},{2,1},{3,0},{4,7},{5,6},{6,5},{7,4},{8,11},{9,10},{10,... | collective-permute-start | bytes 393224 | tf_op jit(solution)/shard_map/ppermute | solution.py:474
  19.6 10.9 %collective-permute-start.4 = (f32[512,128]{1,0:T(8,128)S(1)}, f32[512,128]{1,0:T(8,128)S(1)}, u32[]{:S(2)}, u32[]{:S(2)}) collective-permute-start(f32[512,128]{1,0:T(8,128)S(1)} %get-tuple-element.61), channel_id=1, source_target_pairs={{0,2},{1,3},{2,0},{3,1},{4,6},{5,7},{6,4},{7,5},{8,10},{9,11},{10,... | collective-permute-start | bytes 786440 | tf_op jit(solution)/shard_map/ppermute | solution.py:474
  21.9 14.8 %collective-permute-start.5 = (f32[512,128]{1,0:T(8,128)S(1)}, f32[512,128]{1,0:T(8,128)S(1)}, u32[]{:S(2)}, u32[]{:S(2)}) collective-permute-start(f32[512,128]{1,0:T(8,128)S(1)} %get-tuple-element.62), channel_id=1, source_target_pairs={{0,3},{1,2},{2,1},{3,0},{4,7},{5,6},{6,5},{7,4},{8,11},{9,10},{10,... | collective-permute-start | bytes 786440 | tf_op jit(solution)/shard_map/ppermute | solution.py:474
  27.3 13.3 %collective-permute-start.9 = (f32[128,128]{1,0:T(8,128)S(1)}, f32[128,128]{1,0:T(8,128)S(1)}, u32[]{:S(2)}, u32[]{:S(2)}) collective-permute-start(f32[128,128]{1,0:T(8,128)S(1)} %halo_message.6), channel_id=1, source_target_pairs={{0,4},{1,5},{2,6},{3,7},{4,8},{5,9},{6,10},{7,11},{8,12},{9,13},{1... | collective-permute-start | bytes 196616 | tf_op jit(solution)/shard_map/ppermute | solution.py:471
  37.5 17.2 %collective-permute-start.16 = (f32[1024,128]{1,0:T(8,128)S(1)}, f32[1024,128]{1,0:T(8,128)S(1)}, u32[]{:S(2)}, u32[]{:S(2)}) collective-permute-start(f32[1024,128]{1,0:T(8,128)S(1)} %halo_message.5), channel_id=1, source_target_pairs={{0,4},{1,5},{2,6},{3,7},{4,8},{5,9},{6,10},{7,11},{8,12},{9,13},{1... | collective-permute-start | bytes 1572872 | tf_op jit(solution)/shard_map/ppermute | solution.py:471
  38.9 13.3 %collective-permute-start.14 = (f32[512,128]{1,0:T(8,128)S(1)}, f32[512,128]{1,0:T(8,128)S(1)}, u32[]{:S(2)}, u32[]{:S(2)}) collective-permute-start(f32[512,128]{1,0:T(8,128)S(1)} %get-tuple-element.75), channel_id=1, source_target_pairs={{0,2},{1,3},{2,0},{3,1},{4,6},{5,7},{6,4},{7,5},{8,10},{9,11},{10,... | collective-permute-start | bytes 786440 | tf_op jit(solution)/shard_map/ppermute | solution.py:474
  40.1 12.7 %collective-permute-start.15 = (f32[512,128]{1,0:T(8,128)S(1)}, f32[512,128]{1,0:T(8,128)S(1)}, u32[]{:S(2)}, u32[]{:S(2)}) collective-permute-start(f32[512,128]{1,0:T(8,128)S(1)} %get-tuple-element.76), channel_id=1, source_target_pairs={{0,3},{1,2},{2,1},{3,0},{4,7},{5,6},{6,5},{7,4},{8,11},{9,10},{10,... | collective-permute-start | bytes 786440 | tf_op jit(solution)/shard_map/ppermute | solution.py:474
  50.0 38.3 %collective-permute-start.10 = (f32[960,128]{1,0:T(8,128)S(1)}, f32[960,128]{1,0:T(8,128)S(1)}, u32[]{:S(2)}, u32[]{:S(2)}) collective-permute-start(f32[960,128]{1,0:T(8,128)S(1)} %get-tuple-element.68), channel_id=1, source_target_pairs={{0,12},{1,13},{2,14},{3,15},{4,0},{5,1},{6,2},{7,3},{8,4},{9,5},{1... | collective-permute-start | bytes 1474568 | tf_op jit(solution)/shard_map/ppermute | solution.py:471
  53.7 21.7 %collective-permute-start.21 = (f32[1024,128]{1,0:T(8,128)S(1)}, f32[1024,128]{1,0:T(8,128)S(1)}, u32[]{:S(2)}, u32[]{:S(2)}) collective-permute-start(f32[1024,128]{1,0:T(8,128)S(1)} %halo_message.7), channel_id=1, source_target_pairs={{0,4},{1,5},{2,6},{3,7},{4,8},{5,9},{6,10},{7,11},{8,12},{9,13},{1... | collective-permute-start | bytes 1572872 | tf_op jit(solution)/shard_map/ppermute | solution.py:471
  64.1 27.7 %collective-permute-start.17 = (f32[960,128]{1,0:T(8,128)S(1)}, f32[960,128]{1,0:T(8,128)S(1)}, u32[]{:S(2)}, u32[]{:S(2)}) collective-permute-start(f32[960,128]{1,0:T(8,128)S(1)} %get-tuple-element.80), channel_id=1, source_target_pairs={{0,12},{1,13},{2,14},{3,15},{4,0},{5,1},{6,2},{7,3},{8,4},{9,5},{1... | collective-permute-start | bytes 1474568 | tf_op jit(solution)/shard_map/ppermute | solution.py:471
  84.7 13.6 %collective-permute-start.22 = (f32[960,128]{1,0:T(8,128)S(1)}, f32[960,128]{1,0:T(8,128)S(1)}, u32[]{:S(2)}, u32[]{:S(2)}) collective-permute-start(f32[960,128]{1,0:T(8,128)S(1)} %get-tuple-element.88), channel_id=1, source_target_pairs={{0,12},{1,13},{2,14},{3,15},{4,0},{5,1},{6,2},{7,3},{8,4},{9,5},{1... | collective-permute-start | bytes 1474568 | tf_op jit(solution)/shard_map/ppermute | solution.py:471
  89.2 11.2 %collective-permute-start.11 = (f32[384,128]{1,0:T(8,128)S(1)}, f32[384,128]{1,0:T(8,128)S(1)}, u32[]{:S(2)}, u32[]{:S(2)}) collective-permute-start(f32[384,128]{1,0:T(8,128)S(1)} %get-tuple-element.70), channel_id=1, source_target_pairs={{0,1},{1,0},{2,3},{3,2},{4,5},{5,4},{6,7},{7,6},{8,9},{9,8},{10,11... | collective-permute-start | bytes 589832 | tf_op jit(solution)/shard_map/ppermute | solution.py:474
  90.1 12.3 %collective-permute-start.12 = (f32[384,128]{1,0:T(8,128)S(1)}, f32[384,128]{1,0:T(8,128)S(1)}, u32[]{:S(2)}, u32[]{:S(2)}) collective-permute-start(f32[384,128]{1,0:T(8,128)S(1)} %get-tuple-element.71), channel_id=1, source_target_pairs={{0,2},{1,3},{2,0},{3,1},{4,6},{5,7},{6,4},{7,5},{8,10},{9,11},{10,... | collective-permute-start | bytes 589832 | tf_op jit(solution)/shard_map/ppermute | solution.py:474
  91.3 11.0 %collective-permute-start.13 = (f32[384,128]{1,0:T(8,128)S(1)}, f32[384,128]{1,0:T(8,128)S(1)}, u32[]{:S(2)}, u32[]{:S(2)}) collective-permute-start(f32[384,128]{1,0:T(8,128)S(1)} %get-tuple-element.72), channel_id=1, source_target_pairs={{0,3},{1,2},{2,1},{3,0},{4,7},{5,6},{6,5},{7,4},{8,11},{9,10},{10,... | collective-permute-start | bytes 589832 | tf_op jit(solution)/shard_map/ppermute | solution.py:474
  92.8 10.9 %collective-permute-start.18 = (f32[384,128]{1,0:T(8,128)S(1)}, f32[384,128]{1,0:T(8,128)S(1)}, u32[]{:S(2)}, u32[]{:S(2)}) collective-permute-start(f32[384,128]{1,0:T(8,128)S(1)} %get-tuple-element.82), channel_id=1, source_target_pairs={{0,1},{1,0},{2,3},{3,2},{4,5},{5,4},{6,7},{7,6},{8,9},{9,8},{10,11... | collective-permute-start | bytes 589832 | tf_op jit(solution)/shard_map/ppermute | solution.py:474
  98.3 6.2 %collective-permute-start.19 = (f32[384,128]{1,0:T(8,128)S(1)}, f32[384,128]{1,0:T(8,128)S(1)}, u32[]{:S(2)}, u32[]{:S(2)}) collective-permute-start(f32[384,128]{1,0:T(8,128)S(1)} %get-tuple-element.83), channel_id=1, source_target_pairs={{0,2},{1,3},{2,0},{3,1},{4,6},{5,7},{6,4},{7,5},{8,10},{9,11},{10,... | collective-permute-start | bytes 589832 | tf_op jit(solution)/shard_map/ppermute | solution.py:474
  100.5 9.5 %collective-permute-start.20 = (f32[384,128]{1,0:T(8,128)S(1)}, f32[384,128]{1,0:T(8,128)S(1)}, u32[]{:S(2)}, u32[]{:S(2)}) collective-permute-start(f32[384,128]{1,0:T(8,128)S(1)} %get-tuple-element.84), channel_id=1, source_target_pairs={{0,3},{1,2},{2,1},{3,0},{4,7},{5,6},{6,5},{7,4},{8,11},{9,10},{10,... | collective-permute-start | bytes 589832 | tf_op jit(solution)/shard_map/ppermute | solution.py:474
  102.4 7.6 %collective-permute-start.23 = (f32[384,128]{1,0:T(8,128)S(1)}, f32[384,128]{1,0:T(8,128)S(1)}, u32[]{:S(2)}, u32[]{:S(2)}) collective-permute-start(f32[384,128]{1,0:T(8,128)S(1)} %get-tuple-element.90), channel_id=1, source_target_pairs={{0,1},{1,0},{2,3},{3,2},{4,5},{5,4},{6,7},{7,6},{8,9},{9,8},{10,11... | collective-permute-start | bytes 589832 | tf_op jit(solution)/shard_map/ppermute | solution.py:474
  102.4 10.9 %collective-permute-start.24 = (f32[384,128]{1,0:T(8,128)S(1)}, f32[384,128]{1,0:T(8,128)S(1)}, u32[]{:S(2)}, u32[]{:S(2)}) collective-permute-start(f32[384,128]{1,0:T(8,128)S(1)} %get-tuple-element.91), channel_id=1, source_target_pairs={{0,2},{1,3},{2,0},{3,1},{4,6},{5,7},{6,4},{7,5},{8,10},{9,11},{10,... | collective-permute-start | bytes 589832 | tf_op jit(solution)/shard_map/ppermute | solution.py:474
  103.6 14.2 %collective-permute-start.25 = (f32[384,128]{1,0:T(8,128)S(1)}, f32[384,128]{1,0:T(8,128)S(1)}, u32[]{:S(2)}, u32[]{:S(2)}) collective-permute-start(f32[384,128]{1,0:T(8,128)S(1)} %get-tuple-element.92), channel_id=1, source_target_pairs={{0,3},{1,2},{2,1},{3,0},{4,7},{5,6},{6,5},{7,4},{8,11},{9,10},{10,... | collective-permute-start | bytes 589832 | tf_op jit(solution)/shard_map/ppermute | solution.py:474

commit v2 on v1

--- a/solution.py
+++ b/solution.py
@@ -14,6 +14,7 @@
 PLANE = 4
 HEADS = 3
 HALO = 14
+ATTEND_COST = 1 << 26
 F32 = jnp.float32
 BF16 = jnp.bfloat16
 VMEM = pltpu.VMEM
@@ -82,30 +83,28 @@
     return zero, one, two
 
 
-def pack_first_kernel(info, k_ref, v_ref, *outs):
+def pack_kernel(info, k_ref, v_ref, q_ref, g_ref, *outs):
+    mine, near, far = outs[:2], outs[2:5], outs[5:8]
     lane = lax.broadcasted_iota(jnp.int32, (8, 128), 1)
     meta = jnp.zeros((8, 128), F32)
     for i in range(20):
         meta = jnp.where(lane == i, info[i].astype(F32), meta)
-    for s in range(PLANE):
-        outs[s][pl.ds(ROWS, 8), :] = meta
-        for c in range(CELLS):
-            blocks = head_blocks(info, c, s, k_ref, v_ref, False)
-            outs[s][pl.ds(c * CELL, CELL), :] = blocks[0]()
-
-
-def pack_rest_kernel(info, k_ref, v_ref, q_ref, g_ref, *outs):
-    mine, core, near, far = outs[0], outs[1], outs[2:5], outs[5:8]
-    for s in range(PLANE):
+    for out, row0 in zip((*mine, near[0], far[0]), META_ROWS):
+        out[pl.ds(row0, 8), :] = meta
+    for s in (2, 3, 1, 0):
         for c in range(CELLS):
             kv = head_blocks(info, c, s, k_ref, v_ref, False)
             qg = head_blocks(info, c, s, q_ref, g_ref, True)
-            for i, block in enumerate((kv[1], kv[2], qg[0], qg[1], qg[2])):
+            for h in range(HEADS):
                 if s < 2:
-                    outs[s][pl.ds(i * ROWS + c * CELL, CELL), :] = block()
+                    out, row0 = mine[s], 2 * ROWS * h
                 else:
-                    part, row0 = ((1, 0), (2, 0), (0, 0), (1, ROWS), (2, ROWS))[i]
-                    (near, far)[s - 2][part][pl.ds(row0 + c * CELL, CELL), :] = block()
+                    out, row0 = (near, far)[s - 2][h], 0
+                out[pl.ds(row0 + c * CELL, CELL), :] = kv[h]()
+                out[pl.ds(row0 + ROWS + c * CELL, CELL), :] = qg[h]()
+
+
+META_ROWS = (6 * ROWS, 6 * ROWS, 2 * ROWS, 2 * ROWS)
 
 
 def pack(kernel, shapes, name, info, *arrays):
@@ -131,51 +130,40 @@
             rank = rank + moved.astype(jnp.int32)
 
 
-def halo_kernel(total, kv_rows, qg_rows, with_meta, info, meta, *refs):
-    kv, qg, out = refs[:4], refs[4:-1], refs[-1]
-    queries = 0 if kv_rows is None else HALO
+def halo_kernel(total, h, info, meta, *refs):
+    parts, out = refs[:4], refs[4]
 
     def visit(s, c, rel, slot):
-        if kv_rows is not None:
-
-            @pl.when(rel >= 4)
-            def _():
-                out[cells(slot), :] = kv[s][pl.ds(kv_rows[s] + c * CELL, CELL), :]
-
-        if qg_rows is not None:
-
-            @pl.when(rel >= 16)
-            def _():
-                out[cells(queries + slot - 12), :] = qg[s][pl.ds(qg_rows[s] + c * CELL, CELL), :]
+        @pl.when(rel >= 4)
+        def _():
+            out[cells(slot), :] = parts[s][pl.ds(KV_ROWS[h][s] + c * CELL, CELL), :]
+
+        @pl.when(rel >= 16)
+        def _():
+            out[cells(slot + 2), :] = parts[s][pl.ds(QG_ROWS[h][s] + c * CELL, CELL), :]
 
     walk(meta, info[25], total, visit)
-    if with_meta:
-        out[pl.ds(HALO * CELL, 8), :] = jnp.zeros((8, 128), F32)
+    if h == 0:
+        out[pl.ds((HALO + 2) * CELL, 8), :] = jnp.zeros((8, 128), F32)
         for s in range(PLANE):
-            out[pl.ds(HALO * CELL + s, 1), :] = kv[s][pl.ds(ROWS, 1), :]
-
-
-def halo_message(total, info, meta, kv, qg, with_meta=False):
-    rows, arrays = 0, []
-    if kv is not None:
-        rows += HALO * CELL
-        arrays += [x for x, _ in kv]
-    else:
-        arrays += [x for x, _ in qg]
-    if qg is not None:
-        rows += 2 * CELL
-        arrays += [x for x, _ in qg]
-    rows += 8 if with_meta else 0
-    firsts = [None if x is None else [r for _, r in x] for x in (kv, qg)]
+            out[pl.ds((HALO + 2) * CELL + s, 1), :] = parts[s][pl.ds(META_ROWS[s], 1), :]
+
+
+KV_ROWS = tuple((2 * h * ROWS, 2 * h * ROWS, 0, 0) for h in range(HEADS))
+QG_ROWS = tuple(tuple(r + ROWS for r in rows) for rows in KV_ROWS)
+
+
+def halo_message(total, h, info, meta, parts):
+    rows = (HALO + 2) * CELL + (8 if h == 0 else 0)
     return pl.pallas_call(
-        functools.partial(halo_kernel, total, *firsts, with_meta),
+        functools.partial(halo_kernel, total, h),
         out_shape=jax.ShapeDtypeStruct((rows, 128), F32),
-        in_specs=[sspec()] * 2 + [vspec()] * len(arrays),
+        in_specs=[sspec()] * 2 + [vspec()] * 4,
         out_specs=vspec(),
         compiler_params=params(),
         cost_estimate=cost(1 << 10, 1 << 20),
         name="halo_message",
-    )(info, meta, *arrays)
+    )(info, meta, *parts)
 
 
 def split(x):
@@ -195,11 +183,11 @@
     return lax.dot_general(a, b, (((0,), (0,)), ((), ())), preferred_element_type=F32)
 
 
-def attend_kernel(total, kv_rows, qg_rows, m_row, info, meta, meta_prev, *refs):
-    kv, halo, qg, qgm = refs[:4], refs[4], refs[5:9], refs[9]
-    dkv, dq, back = refs[10:13]
-    kcat, vcat, kt, acc_k, acc_v, qcat, gcat, qrhs, grhs, dq_scr = refs[13:23]
-    pairs = (refs[23:25], refs[25:27])
+def attend_kernel(total, h, info, meta, meta_prev, *refs):
+    here_parts, halo = refs[:4], refs[4]
+    dkv, dq, back = refs[5:8]
+    kcat, vcat, kt, acc_k, acc_v, qcat, gcat, qrhs, grhs, dq_scr = refs[8:18]
+    pairs = (refs[18:20], refs[20:22])
     start = info[25]
     start_prev = info[26]
     lane = lax.broadcasted_iota(jnp.int32, (CELL, 128), 1)
@@ -243,8 +231,8 @@
 
     def own(s, c, rel, slot):
         here = rel < 16
-        put_key(kv[s][pl.ds(kv_rows[s] + c * CELL, CELL), :], jnp.where(here, 12 + rel, 28), meta, s, c)
-        put_query(qg[s][pl.ds(qg_rows[s] + c * CELL, CELL), :], jnp.where(here, rel, 16))
+        put_key(here_parts[s][pl.ds(KV_ROWS[h][s] + c * CELL, CELL), :], jnp.where(here, 12 + rel, 28), meta, s, c)
+        put_query(here_parts[s][pl.ds(QG_ROWS[h][s] + c * CELL, CELL), :], jnp.where(here, rel, 16))
 
     walk(meta, start, total, own)
     came = [jnp.int32(0), jnp.int32(0)]
@@ -258,7 +246,7 @@
 
     walk(meta_prev, start_prev, total, before)
     for i in range(2):
-        put_query(qgm[pl.ds(m_row + i * CELL, CELL), :], came[i])
+        put_query(halo[pl.ds((HALO + i) * CELL, CELL), :], came[i])
     for j in range(7):
         kt[:, pl.ds(j * ROWS, ROWS)] = kcat[pl.ds(j * ROWS, ROWS), pl.ds(0, 128)].T
     acc_k[...] = jnp.zeros(acc_k.shape, F32)
@@ -341,15 +329,13 @@
     back[pl.ds(HALO * CELL, CELL), :] = pair
 
 
-def attend(total, info, meta, meta_prev, kv, halo, qg, qgm, m_row):
-    kv_rows, qg_rows = ([r for _, r in x] for x in (kv, qg))
-    kv, qg = ([x for x, _ in y] for y in (kv, qg))
+def attend(total, h, info, meta, meta_prev, parts, halo):
     shapes = [(4 * ROWS, 128), (2 * ROWS, 128), (HALO * CELL + CELL, 128)]
     keys, queries = 29 * CELL, 17 * CELL
     return pl.pallas_call(
-        functools.partial(attend_kernel, total, kv_rows, qg_rows, m_row),
+        functools.partial(attend_kernel, total, h),
         out_shape=[jax.ShapeDtypeStruct(s, F32) for s in shapes],
-        in_specs=[sspec()] * 3 + [vspec()] * 10,
+        in_specs=[sspec()] * 3 + [vspec()] * 5,
         out_specs=[vspec()] * 3,
         scratch_shapes=[
             VMEM((keys, 512), BF16),
@@ -365,15 +351,18 @@
         ]
         + [VMEM((4 * ROWS, ROWS), F32)] * 4,
         compiler_params=params(24),
-        cost_estimate=cost(8 << 30, 8 << 20),
+        cost_estimate=cost(ATTEND_COST, 1 << 20),
         name="attend",
-    )(info, meta, meta_prev, *kv, halo, *qg, qgm)
+    )(info, meta, meta_prev, *parts, halo)
 
 
 OUT = ROWS + ROWS // 2
 
 
-def finish_kernel(total, info, meta, dkv, dq, back, *outs):
+def finish_kernel(total, n, info, meta, dkv, dq, back, *refs):
+    earlier, outs = refs[:n], refs[n:]
+    for i in range(n):
+        outs[1][pl.ds((i + 1) * OUT, OUT), :] = earlier[i][...]
     low = lanes((CELL, 128)) < 64
     pair = back[pl.ds(HALO * CELL, CELL), :]
     for s in range(PLANE):
@@ -395,34 +384,42 @@
     walk(meta, info[25], total, visit)
 
 
-def finish(total, info, meta, dkv, dq, back):
-    shapes = [(OUT, 128)] * 4
+def finish(total, info, meta, dkv, dq, back, earlier):
+    n = len(earlier)
+    shapes = [(OUT, 128), (OUT * (n + 1), 128), (OUT, 128), (OUT, 128)]
     return pl.pallas_call(
-        functools.partial(finish_kernel, total),
+        functools.partial(finish_kernel, total, n),
         out_shape=[jax.ShapeDtypeStruct(s, F32) for s in shapes],
-        in_specs=[sspec()] * 2 + [vspec()] * 3,
+        in_specs=[sspec()] * 2 + [vspec()] * (3 + n),
         out_specs=[vspec()] * 4,
         compiler_params=params(),
         cost_estimate=cost(1 << 10, 2 << 20),
         name="finish",
-    )(info, meta, dkv, dq, back)
+    )(info, meta, dkv, dq, back, *earlier)
 
 
 def unpack_kernel(info, *refs):
-    parts, (oq, ok, ov) = refs[:12], refs[12:]
+    core, heads, (oq, ok, ov) = refs[0], refs[1:10], refs[10:]
     me = info[24]
+    core_row = (OUT, 2 * OUT, 0)
+    step = pl.program_id(0)
+
+    def rows(s, h, row):
+        if s == 1:
+            return core[pl.ds(pl.multiple_of(core_row[h] + row, CELL), CELL), :]
+        return heads[3 * h + (0, None, 1, 2)[s]][pl.ds(pl.multiple_of(row, CELL), CELL), :]
 
     def grads(s, c, h):
-        return parts[4 * h + s][pl.ds(c * CELL, CELL), :]
+        return rows(s, h, (2 * step + c) * CELL)
 
     def query(s, c, h):
-        x = parts[4 * h + s][pl.ds(ROWS + (c // 2) * CELL, CELL), :]
+        x = rows(s, h, ROWS + step * CELL)
         return x, swap_half(x)
 
     for s in range(PLANE):
         j = lax.bitwise_xor(me, s)
         first = pl.ds(pl.multiple_of(j * 128, 128), 128)
-        for c in range(CELLS):
+        for c in range(2):
             r = pl.ds(c * CELL, CELL)
             a, b = grads(s, c, 0), grads(s, c, 1)
             ok[r, first] = join(a, swap_half(b))
@@ -434,7 +431,7 @@
         j = lax.bitwise_xor(me, s)
         even = (j % 2) == 0
         last = pl.ds(pl.multiple_of((4 + j // 2) * 128, 128), 128)
-        for c in range(CELLS):
+        for c in range(2):
             r = pl.ds(c * CELL, CELL)
             u, w = grads(s, c, 2), grads(s + 1, c, 2)
             a, b = jnp.where(even, u, w), jnp.where(even, w, u)
@@ -445,16 +442,17 @@
             oq[r, last] = join(a, swap_half(b)) if c % 2 == 0 else join(swap_half(a), b)
 
 
-def unpack_heads(info, parts, features):
+def unpack_heads(info, core, parts, features):
     return pl.pallas_call(
         unpack_kernel,
         out_shape=[jax.ShapeDtypeStruct((ROWS, features), F32)] * 3,
-        in_specs=[sspec()] + [vspec()] * 12,
-        out_specs=[vspec()] * 3,
+        grid=(2,),
+        in_specs=[sspec()] + [vspec()] * 10,
+        out_specs=[pl.BlockSpec((ROWS // 2, features), lambda i: (i, 0))] * 3,
         compiler_params=params(),
         cost_estimate=cost(1 << 20, 5 << 20),
         name="unpack_heads",
-    )(info, *[x for part in parts for x in part])
+    )(info, core, *[x for part in parts for x in part])
 
 
 def after(x, *earlier):
@@ -478,63 +476,54 @@
     tail = jnp.stack([jnp.int32(0)] * 4 + [index % PLANE, start, start_prev, jnp.int32(0)])
     info = jnp.concatenate([placement, cell_lengths, gene_mask.reshape(-1), tail])
 
-    own0, core0, near0, far0 = pack(
-        pack_first_kernel, [(ROWS + 8, 128)] * 4, "pack_first", info, key_rows, value_rows
-    )
-    near0, far0, core0 = swap(near0, 2), swap(far0, 3), swap(core0, 1)
-    sizes = [5 * ROWS] * 2 + [ROWS, 2 * ROWS, 2 * ROWS] * 2
-    own, core, *rest = pack(
-        pack_rest_kernel,
-        [(n, 128) for n in sizes],
-        "pack_rest",
-        after(info, own0),
-        key_rows,
-        value_rows,
-        query_rows,
-        grad_rows,
-    )
+    sizes = [6 * ROWS + 8] * 2 + [2 * ROWS + 8, 2 * ROWS, 2 * ROWS] * 2
+    shapes = [(n, 128) for n in sizes]
+    arrays = (key_rows, value_rows, query_rows, grad_rows)
+    own, core, *rest = pack(pack_kernel, shapes, "pack_heads", info, *arrays)
     near, far = rest[:3], rest[3:]
 
-    def across(i, *earlier):
-        pair = (near[i], far[i])
+    def across(h, *earlier):
+        pair = (near[h], far[h])
         if earlier:
             pair = after(pair, *earlier)
-        near[i], far[i] = swap(pair[0], 2), swap(pair[1], 3)
+        near[h], far[h] = swap(pair[0], 2), swap(pair[1], 3)
 
     across(0)
-    first = after((core0, near0, far0), own)
-    kv0 = [(x, 0) for x in (own0, *first)]
-    meta = jnp.stack([x[ROWS, :32] for x, _ in kv0]).astype(jnp.int32)
-    message0 = halo_message(total, info, meta, kv0, None, True)
-    halo0 = along_z(message0, 1)
-    core = swap(after(core, *first), 1)
-    across(1, message0)
-
-    def sources(row0, i, row1):
-        return [(own, row0), (core, row0), (near[i], row1), (far[i], row1)]
-
-    qg0 = sources(2 * ROWS, 0, 0)
-    movers0 = halo_message(total, info, meta, None, qg0)
-    qgm0 = along_z(movers0, 1)
-    across(2, movers0)
-    kv = [kv0, sources(0, 1, 0), sources(ROWS, 2, 0)]
-    qg = [qg0, sources(3 * ROWS, 1, ROWS), sources(4 * ROWS, 2, ROWS)]
-    messages = [message0] + [halo_message(total, info, meta, kv[h], qg[h]) for h in (1, 2)]
-    halo = [halo0] + [along_z(messages[h], 1) for h in (1, 2)]
-    movers = [(qgm0, 0), (halo[1], HALO * CELL), (halo[2], HALO * CELL)]
-    meta_prev = halo0[HALO * CELL : HALO * CELL + 4, :32].astype(jnp.int32)
-
-    parts = []
-    turn = ()
+    core = swap(core, 1)
+    across(1, core)
+    first = (own, core, near[0], far[0])
+    meta = jnp.stack([x[r, :32] for x, r in zip(first, META_ROWS)]).astype(jnp.int32)
+    message = halo_message(total, 0, info, meta, first)
+    halo = [along_z(message, 1)]
+    across(2, message)
+    corner = (HALO + 2) * CELL
+    meta_prev = halo[0][corner : corner + 4, :32].astype(jnp.int32)
+    dkv, dq, back = [], [], []
     for h in range(HEADS):
-        came, m_row = movers[h]
-        sent = messages[h + 1 :][:1]
-        info_h = after(info, *turn, *sent)
-        dkv, dq, back = attend(total, info_h, meta, meta_prev, kv[h], halo[h], qg[h], came, m_row)
-        turn = (dq,)
-        mine, *outs = finish(total, info, meta, dkv, dq, along_z(back, -1))
-        parts.append([mine] + [swap(x, i + 1) for i, x in enumerate(outs)])
-    return tuple(unpack_heads(info, parts, query_rows.shape[1]))
+        earlier = [*dq[-1:], message]
+        if h < HEADS - 1:
+            held = (own, core, near[h + 1], far[h + 1])
+            message = halo_message(total, h + 1, after(info, *dq[-1:]), meta, held)
+            halo.append(along_z(message, 1))
+            earlier.append(message)
+        held = (own, core, near[h], far[h])
+        outs = attend(total, h, after(info, *earlier), meta, meta_prev, held, halo[h])
+        dkv.append(outs[0])
+        dq.append(outs[1])
+        back.append(along_z(outs[2], -1))
+
+    parts, cores = [], []
+
+    def finish_head(h):
+        earlier = cores[:] if h == HEADS - 1 else []
+        info_h = after(info, *(parts[-1][1:] if parts else dq[2:]))
+        mine, core, near, far = finish(total, info_h, meta, dkv[h], dq[h], back[h], earlier)
+        cores.append(core)
+        parts.append((mine, swap(near, 2), swap(far, 3)))
+
+    for h in range(HEADS):
+        finish_head(h)
+    return tuple(unpack_heads(info, swap(cores[-1], 1), parts, query_rows.shape[1]))
 
 
 def solution(mesh):

time: 121 us -> 118 us (0.975)
  starting transfers between devices: 33.4 us -> 20.2 us
  waiting for transfers between devices: 43.3 us -> 52.9 us
  local copies, waits for them, and re-layouts: 3.79 us -> 6.04 us
  Pallas kernels: 39.1 us -> 37.5 us
    ppermute x19 -> x14, waiting for transfers between devices: 27.8 us -> 50.2 us  [swap(): return lax.ppermute(x, 'ctx', [(i, i ^ bit) for i in range(count)])]
    ppermute x7 -> x6, waiting for transfers between devices: 15.5 us -> 2.75 us  [along_z(): lax.ppermute(x, 'ctx', [(i, (i + step * PLANE) % count) for i in range(co...]
    ppermute x19 -> x14, starting transfers between devices: 20 us -> 13.1 us  [swap(): return lax.ppermute(x, 'ctx', [(i, i ^ bit) for i in range(count)])]
    ppermute x7 -> x6, starting transfers between devices: 13.4 us -> 7.03 us  [along_z(): lax.ppermute(x, 'ctx', [(i, (i + step * PLANE) % count) for i in range(co...]
    unnamed x14, local copies, waits for them, and re-layouts: 3.62 us -> 5.87 us
    pallas_call x10 -> x9, Pallas kernels: 34.2 us -> 33.5 us  [the longest x3 28.1 us: attend(): pl.pallas_call(functools.partial(attend_kernel, total, h), out_shape=[jax...]
  transfers between devices with their start and end apart: 26 -> 20, of which waited for: 13 -> 13; matrix products, arithmetic and copies ran while one was open for 0% -> 0% of each run, Pallas kernels for 30% -> 27%
where the time goes in v2:
time: 118 us; the launch traced here: 117 us
  waiting for transfers between devices  52.9 us (45%)
  Pallas kernels  37.5 us (32%)
  starting transfers between devices  20.2 us (17%)
  local copies, waits for them, and re-layouts  6.04 us (5%)
    ppermute x14, waiting for transfers between devices, swap(): return lax.ppermute(x, 'ctx', [(i, i ^ bit) for i in range(count)])  50.2 us
    pallas_call x3, Pallas kernels, attend(): pl.pallas_call(functools.partial(attend_kernel, total, h), out_shape=[jax...  28.1 us
    ppermute x14, starting transfers between devices, swap(): return lax.ppermute(x, 'ctx', [(i, i ^ bit) for i in range(count)])  13.1 us
    ppermute x6, starting transfers between devices, along_z(): lax.ppermute(x, 'ctx', [(i, (i + step * PLANE) % count) for i in range(co...  7.03 us
    unnamed x14, local copies, waits for them, and re-layouts  5.87 us
    pallas_call x3, Pallas kernels, finish(): pl.pallas_call(functools.partial(finish_kernel, total, n), out_shape=[jax...  2.84 us
    ppermute x6, waiting for transfers between devices, along_z(): lax.ppermute(x, 'ctx', [(i, (i + step * PLANE) % count) for i in range(co...  2.75 us
    pallas_call x3, Pallas kernels, halo_message(): pl.pallas_call(functools.partial(halo_kernel, total, h), out_shape=jax.Sh...  2.54 us
  transfers between devices with their start and end apart: 20, of which 13 were waited for; matrix products, arithmetic and copies ran while one was open for 0% of the time, Pallas kernels for 27%

profile of v2, /device:TPU:1, one launch (start us, length us, event | category | flops | bytes accessed | tf_op | source)
XLA Modules:
  0.0 117.4 jit_solution(10583105407840252919)
XLA Ops:
  0.7 0.0 copy-start.4
  0.7 0.7 copy-done.4
  1.3 0.1 reshape.9
  1.4 0.0 copy-start.5
  1.4 0.0 copy-start.6
  1.4 0.7 copy-done.5
  2.1 0.0 copy-done.6
  2.1 0.1 concatenate.3.info
  2.2 0.0 copy-start
  2.2 1.1 copy-done
  3.3 1.1 copy-done.1
  4.4 1.1 copy-done.2
  5.6 1.1 copy-done.3
  6.7 1.7 %pack_heads.1 = (f32[1544,128]{1,0:T(8,128)S(1)}, f32[1544,128]{1,0:T(8,128)S(1)}, f32[520,128]{1,0:T(8,128)S(1)}, f32[512,128]{1,0:T(8,128)S(1)}, f32[512,128]{...) custom-call(s32[28]{0:T(128)S(1)} %concatenate.3.info, ...), custom_call_target="tpu_custom_call" | custom-call | flops 1048576 | bytes 3145728 | tf_op jit(solution)/shard_map/pack_heads/pallas_call | solution.py:111
  8.4 0.1 collective-permute-start
  8.6 2.7 %collective-permute-start.1 = (f32[520,128]{1,0:T(8,128)S(1)}, f32[520,128]{1,0:T(8,128)S(1)}, u32[]{:S(2)}, u32[]{:S(2)}) collective-permute-start(f32[520,128]{1,0:T(8,128)S(1)} %get-tuple-element.45), channel_id=1, source_target_pairs={{0,2},{1,3},{2,0},{3,1},{4,6},{5,7},{6,4},{7,5},{8,10},{9,11},{10,... | collective-permute-start | bytes 798728 | tf_op jit(solution)/shard_map/ppermute | solution.py:472
  11.2 0.0 collective-permute-start.2
  11.3 6.6 %collective-permute-done.1.refs_2_ = f32[520,128]{1,0:T(8,128)S(1)} collective-permute-done((f32[520,128]{1,0:T(8,128)S(1)}, f32[520,128]{1,0:T(8,128)S(1)}, u32[]{:S(2)}, u32[]{:S(2)}) %collective-permute-start.1) | collective-permute-done | bytes 266272 | tf_op jit(solution)/shard_map/ppermute | solution.py:472
  17.9 5.7 %collective-permute-done.2.refs_3_ = f32[520,128]{1,0:T(8,128)S(1)} collective-permute-done((f32[520,128]{1,0:T(8,128)S(1)}, f32[520,128]{1,0:T(8,128)S(1)}, u32[]{:S(2)}, u32[]{:S(2)}) %collective-permute-start.2) | collective-permute-done | bytes 266272 | tf_op jit(solution)/shard_map/ppermute | solution.py:472
  23.6 0.0 collective-permute-done.refs_1_
  23.7 0.8 halo_message.3
  24.5 1.6 %collective-permute-start.5 = (f32[1032,128]{1,0:T(8,128)S(1)}, f32[1032,128]{1,0:T(8,128)S(1)}, u32[]{:S(2)}, u32[]{:S(2)}) collective-permute-start(f32[1032,128]{1,0:T(8,128)S(1)} %halo_message.3), channel_id=1, source_target_pairs={{0,4},{1,5},{2,6},{3,7},{4,8},{5,9},{6,10},{7,11},{8,12},{9,13},{1... | collective-permute-start | bytes 1585160 | tf_op jit(solution)/shard_map/ppermute | solution.py:469
  26.1 1.2 %collective-permute-start.3 = (f32[512,128]{1,0:T(8,128)S(1)}, f32[512,128]{1,0:T(8,128)S(1)}, u32[]{:S(2)}, u32[]{:S(2)}) collective-permute-start(f32[512,128]{1,0:T(8,128)S(1)} %get-tuple-element.49), channel_id=1, source_target_pairs={{0,2},{1,3},{2,0},{3,1},{4,6},{5,7},{6,4},{7,5},{8,10},{9,11},{10,... | collective-permute-start | bytes 786440 | tf_op jit(solution)/shard_map/ppermute | solution.py:472
  27.3 0.9 collective-permute-start.4
  28.2 1.2 %collective-permute-start.6 = (f32[512,128]{1,0:T(8,128)S(1)}, f32[512,128]{1,0:T(8,128)S(1)}, u32[]{:S(2)}, u32[]{:S(2)}) collective-permute-start(f32[512,128]{1,0:T(8,128)S(1)} %get-tuple-element.56), channel_id=1, source_target_pairs={{0,2},{1,3},{2,0},{3,1},{4,6},{5,7},{6,4},{7,5},{8,10},{9,11},{10,... | collective-permute-start | bytes 786440 | tf_op jit(solution)/shard_map/ppermute | solution.py:472
  29.4 0.3 collective-permute-start.7
  29.8 3.7 %collective-permute-done.3.refs_2_ = f32[512,128]{1,0:T(8,128)S(1)} collective-permute-done((f32[512,128]{1,0:T(8,128)S(1)}, f32[512,128]{1,0:T(8,128)S(1)}, u32[]{:S(2)}, u32[]{:S(2)}) %collective-permute-start.3) | collective-permute-done | bytes 262176 | tf_op jit(solution)/shard_map/ppermute | solution.py:472
  33.4 7.3 %collective-permute-done.4.refs_3_ = f32[512,128]{1,0:T(8,128)S(1)} collective-permute-done((f32[512,128]{1,0:T(8,128)S(1)}, f32[512,128]{1,0:T(8,128)S(1)}, u32[]{:S(2)}, u32[]{:S(2)}) %collective-permute-start.4) | collective-permute-done | bytes 262176 | tf_op jit(solution)/shard_map/ppermute | solution.py:472
  40.7 0.8 halo_message.4
  41.5 1.3 %collective-permute-start.8 = (f32[1024,128]{1,0:T(8,128)S(1)}, f32[1024,128]{1,0:T(8,128)S(1)}, u32[]{:S(2)}, u32[]{:S(2)}) collective-permute-start(f32[1024,128]{1,0:T(8,128)S(1)} %halo_message.4), channel_id=1, source_target_pairs={{0,4},{1,5},{2,6},{3,7},{4,8},{5,9},{6,10},{7,11},{8,12},{9,13},{1... | collective-permute-start | bytes 1572872 | tf_op jit(solution)/shard_map/ppermute | solution.py:469
  42.9 0.0 collective-permute-done.5.refs_4_
  42.9 9.4 %attend.3 = (f32[1024,128]{1,0:T(8,128)S(1)}, f32[512,128]{1,0:T(8,128)S(1)}, f32[960,128]{1,0:T(8,128)S(1)}) custom-call(s32[28]{0:T(128)S(1)} %concatenate.3.info, s32[4,32]{1,0:T(4,128)S(1)} %maximum_convert_fusion.meta, s32[4,32]{1,0:T(4,128)S(1)} %slice_convert_fusion.meta_prev, f32[1544,128]{1,0:T(8,128)S(1)} %get-tuple-element.43.refs_0_, ...), custom_call_target="tpu_custom_call" | custom-call | flops 67108864 | bytes 1048576 | tf_op jit(solution)/shard_map/attend/pallas_call | solution.py:335
  52.3 0.0 collective-permute-done.6.refs_2_
  52.3 0.0 collective-permute-done.7.refs_3_
  52.3 0.8 halo_message.5
  53.1 1.3 %collective-permute-start.9 = (f32[1024,128]{1,0:T(8,128)S(1)}, f32[1024,128]{1,0:T(8,128)S(1)}, u32[]{:S(2)}, u32[]{:S(2)}) collective-permute-start(f32[1024,128]{1,0:T(8,128)S(1)} %halo_message.5), channel_id=1, source_target_pairs={{0,4},{1,5},{2,6},{3,7},{4,8},{5,9},{6,10},{7,11},{8,12},{9,13},{1... | collective-permute-start | bytes 1572872 | tf_op jit(solution)/shard_map/ppermute | solution.py:469
  54.5 2.0 %collective-permute-start.10 = (f32[960,128]{1,0:T(8,128)S(1)}, f32[960,128]{1,0:T(8,128)S(1)}, u32[]{:S(2)}, u32[]{:S(2)}) collective-permute-start(f32[960,128]{1,0:T(8,128)S(1)} %get-tuple-element.64), channel_id=1, source_target_pairs={{0,12},{1,13},{2,14},{3,15},{4,0},{5,1},{6,2},{7,3},{8,4},{9,5},{1... | collective-permute-start | bytes 1474568 | tf_op jit(solution)/shard_map/ppermute | solution.py:469
  56.5 0.7 collective-permute-done.8.refs_4_
  57.1 9.4 %attend.4 = (f32[1024,128]{1,0:T(8,128)S(1)}, f32[512,128]{1,0:T(8,128)S(1)}, f32[960,128]{1,0:T(8,128)S(1)}) custom-call(s32[28]{0:T(128)S(1)} %concatenate.3.info, s32[4,32]{1,0:T(4,128)S(1)} %maximum_convert_fusion.meta, s32[4,32]{1,0:T(4,128)S(1)} %slice_convert_fusion.meta_prev, f32[1544,128]{1,0:T(8,128)S(1)} %get-tuple-element.43.refs_0_, ...), custom_call_target="tpu_custom_call" | custom-call | flops 67108864 | bytes 1048576 | tf_op jit(solution)/shard_map/attend/pallas_call | solution.py:335
  66.5 0.6 collective-permute-start.13
  67.1 1.5 %collective-permute-done.9.refs_4_ = f32[1024,128]{1,0:T(8,128)S(1)} collective-permute-done((f32[1024,128]{1,0:T(8,128)S(1)}, f32[1024,128]{1,0:T(8,128)S(1)}, u32[]{:S(2)}, u32[]{:S(2)}) %collective-permute-start.9) | collective-permute-done | bytes 524320 | tf_op jit(solution)/shard_map/ppermute | solution.py:469
  68.5 9.4 %attend.5 = (f32[1024,128]{1,0:T(8,128)S(1)}, f32[512,128]{1,0:T(8,128)S(1)}, f32[960,128]{1,0:T(8,128)S(1)}) custom-call(s32[28]{0:T(128)S(1)} %concatenate.3.info, s32[4,32]{1,0:T(4,128)S(1)} %maximum_convert_fusion.meta, s32[4,32]{1,0:T(4,128)S(1)} %slice_convert_fusion.meta_prev, f32[1544,128]{1,0:T(8,128)S(1)} %get-tuple-element.43.refs_0_, ...), custom_call_target="tpu_custom_call" | custom-call | flops 67108864 | bytes 1048576 | tf_op jit(solution)/shard_map/attend/pallas_call | solution.py:335
  77.9 0.2 collective-permute-start.16
  78.1 0.6 collective-permute-done.10.back
  78.7 0.9 finish.3
  79.7 1.5 %collective-permute-start.11 = (f32[384,128]{1,0:T(8,128)S(1)}, f32[384,128]{1,0:T(8,128)S(1)}, u32[]{:S(2)}, u32[]{:S(2)}) collective-permute-start(f32[384,128]{1,0:T(8,128)S(1)} %get-tuple-element.65), channel_id=1, source_target_pairs={{0,2},{1,3},{2,0},{3,1},{4,6},{5,7},{6,4},{7,5},{8,10},{9,11},{10,... | collective-permute-start | bytes 589832 | tf_op jit(solution)/shard_map/ppermute | solution.py:472
  81.2 1.3 %collective-permute-start.12 = (f32[384,128]{1,0:T(8,128)S(1)}, f32[384,128]{1,0:T(8,128)S(1)}, u32[]{:S(2)}, u32[]{:S(2)}) collective-permute-start(f32[384,128]{1,0:T(8,128)S(1)} %get-tuple-element.66), channel_id=1, source_target_pairs={{0,3},{1,2},{2,1},{3,0},{4,7},{5,6},{6,5},{7,4},{8,11},{9,10},{10,... | collective-permute-start | bytes 589832 | tf_op jit(solution)/shard_map/ppermute | solution.py:472
  82.5 3.1 %collective-permute-done.11.refs_2_ = f32[384,128]{1,0:T(8,128)S(1)} collective-permute-done((f32[384,128]{1,0:T(8,128)S(1)}, f32[384,128]{1,0:T(8,128)S(1)}, u32[]{:S(2)}, u32[]{:S(2)}) %collective-permute-start.11) | collective-permute-done | bytes 196640 | tf_op jit(solution)/shard_map/ppermute | solution.py:472
  85.6 5.3 %collective-permute-done.12.refs_3_ = f32[384,128]{1,0:T(8,128)S(1)} collective-permute-done((f32[384,128]{1,0:T(8,128)S(1)}, f32[384,128]{1,0:T(8,128)S(1)}, u32[]{:S(2)}, u32[]{:S(2)}) %collective-permute-start.12) | collective-permute-done | bytes 196640 | tf_op jit(solution)/shard_map/ppermute | solution.py:472
  90.9 0.0 collective-permute-done.13.back
  90.9 0.9 finish.4
  91.8 1.5 %collective-permute-start.14 = (f32[384,128]{1,0:T(8,128)S(1)}, f32[384,128]{1,0:T(8,128)S(1)}, u32[]{:S(2)}, u32[]{:S(2)}) collective-permute-start(f32[384,128]{1,0:T(8,128)S(1)} %get-tuple-element.70), channel_id=1, source_target_pairs={{0,2},{1,3},{2,0},{3,1},{4,6},{5,7},{6,4},{7,5},{8,10},{9,11},{10,... | collective-permute-start | bytes 589832 | tf_op jit(solution)/shard_map/ppermute | solution.py:472
  93.4 0.0 collective-permute-start.15
  93.4 5.2 %collective-permute-done.14.refs_5_ = f32[384,128]{1,0:T(8,128)S(1)} collective-permute-done((f32[384,128]{1,0:T(8,128)S(1)}, f32[384,128]{1,0:T(8,128)S(1)}, u32[]{:S(2)}, u32[]{:S(2)}) %collective-permute-start.14) | collective-permute-done | bytes 196640 | tf_op jit(solution)/shard_map/ppermute | solution.py:472
  98.6 4.2 %collective-permute-done.15.refs_6_ = f32[384,128]{1,0:T(8,128)S(1)} collective-permute-done((f32[384,128]{1,0:T(8,128)S(1)}, f32[384,128]{1,0:T(8,128)S(1)}, u32[]{:S(2)}, u32[]{:S(2)}) %collective-permute-start.15) | collective-permute-done | bytes 196640 | tf_op jit(solution)/shard_map/ppermute | solution.py:472
  102.8 0.0 collective-permute-done.16.back
  102.8 1.0 finish.5
  103.8 0.5 collective-permute-start.17
  104.2 1.3 %collective-permute-start.18 = (f32[384,128]{1,0:T(8,128)S(1)}, f32[384,128]{1,0:T(8,128)S(1)}, u32[]{:S(2)}, u32[]{:S(2)}) collective-permute-start(f32[384,128]{1,0:T(8,128)S(1)} %get-tuple-element.81), channel_id=1, source_target_pairs={{0,2},{1,3},{2,0},{3,1},{4,6},{5,7},{6,4},{7,5},{8,10},{9,11},{10,... | collective-permute-start | bytes 589832 | tf_op jit(solution)/shard_map/ppermute | solution.py:472
  105.5 0.5 collective-permute-start.19
  106.0 4.7 %collective-permute-done.18.refs_8_ = f32[384,128]{1,0:T(8,128)S(1)} collective-permute-done((f32[384,128]{1,0:T(8,128)S(1)}, f32[384,128]{1,0:T(8,128)S(1)}, u32[]{:S(2)}, u32[]{:S(2)}) %collective-permute-start.18) | collective-permute-done | bytes 196640 | tf_op jit(solution)/shard_map/ppermute | solution.py:472
  110.7 4.4 %collective-permute-done.19.refs_9_ = f32[384,128]{1,0:T(8,128)S(1)} collective-permute-done((f32[384,128]{1,0:T(8,128)S(1)}, f32[384,128]{1,0:T(8,128)S(1)}, u32[]{:S(2)}, u32[]{:S(2)}) %collective-permute-start.19) | collective-permute-done | bytes 196640 | tf_op jit(solution)/shard_map/ppermute | solution.py:472
  115.1 0.0 collective-permute-done.17.refs_0_
  115.1 2.3 %unpack_heads.1 = (f32[256,768]{1,0:T(8,128)}, f32[256,768]{1,0:T(8,128)}, f32[256,768]{1,0:T(8,128)}) custom-call(s32[28]{0:T(128)S(1)} %concatenate.3.info, f32[1152,128]{1,0:T(8,128)S(1)} %collective-permute-done.17.refs_0_, f32[384,128]{1,0:T(8,128)S(1)} %get-tuple-element.78.refs_1_, f32[384,128]{1,0:T(8,128)S(1)} %collective-permute-done.11.refs_2_, ...), custom_call_target="tpu_custom_call" | custom-call | flops 1048576 | bytes 5242880 | tf_op jit(solution)/shard_map/unpack_heads/pallas_call | solution.py:446
  (10 shorter events, 0.0 us)
Async XLA Ops:
  0.7 0.7 copy-start.4
  1.4 0.7 copy-start.5
  1.4 0.7 copy-start.6
  2.2 1.1 copy-start
  3.3 1.1 copy-start.1
  4.4 1.1 copy-start.2
  5.6 1.1 copy-start.3
  8.4 15.2 %collective-permute-start = (f32[1544,128]{1,0:T(8,128)S(1)}, f32[1544,128]{1,0:T(8,128)S(1)}, u32[]{:S(2)}, u32[]{:S(2)}) collective-permute-start(f32[1544,128]{1,0:T(8,128)S(1)} %get-tuple-element.44), channel_id=1, source_target_pairs={{0,1},{1,0},{2,3},{3,2},{4,5},{5,4},{6,7},{7,6},{8,9},{9,8},{10,11... | collective-permute-start | bytes 2371592 | tf_op jit(solution)/shard_map/ppermute | solution.py:472
  8.6 9.4 %collective-permute-start.1 = (f32[520,128]{1,0:T(8,128)S(1)}, f32[520,128]{1,0:T(8,128)S(1)}, u32[]{:S(2)}, u32[]{:S(2)}) collective-permute-start(f32[520,128]{1,0:T(8,128)S(1)} %get-tuple-element.45), channel_id=1, source_target_pairs={{0,2},{1,3},{2,0},{3,1},{4,6},{5,7},{6,4},{7,5},{8,10},{9,11},{10,... | collective-permute-start | bytes 798728 | tf_op jit(solution)/shard_map/ppermute | solution.py:472
  11.2 12.4 %collective-permute-start.2 = (f32[520,128]{1,0:T(8,128)S(1)}, f32[520,128]{1,0:T(8,128)S(1)}, u32[]{:S(2)}, u32[]{:S(2)}) collective-permute-start(f32[520,128]{1,0:T(8,128)S(1)} %get-tuple-element.46), channel_id=1, source_target_pairs={{0,3},{1,2},{2,1},{3,0},{4,7},{5,6},{6,5},{7,4},{8,11},{9,10},{10,... | collective-permute-start | bytes 798728 | tf_op jit(solution)/shard_map/ppermute | solution.py:472
  24.5 18.4 %collective-permute-start.5 = (f32[1032,128]{1,0:T(8,128)S(1)}, f32[1032,128]{1,0:T(8,128)S(1)}, u32[]{:S(2)}, u32[]{:S(2)}) collective-permute-start(f32[1032,128]{1,0:T(8,128)S(1)} %halo_message.3), channel_id=1, source_target_pairs={{0,4},{1,5},{2,6},{3,7},{4,8},{5,9},{6,10},{7,11},{8,12},{9,13},{1... | collective-permute-start | bytes 1585160 | tf_op jit(solution)/shard_map/ppermute | solution.py:469
  26.1 7.4 %collective-permute-start.3 = (f32[512,128]{1,0:T(8,128)S(1)}, f32[512,128]{1,0:T(8,128)S(1)}, u32[]{:S(2)}, u32[]{:S(2)}) collective-permute-start(f32[512,128]{1,0:T(8,128)S(1)} %get-tuple-element.49), channel_id=1, source_target_pairs={{0,2},{1,3},{2,0},{3,1},{4,6},{5,7},{6,4},{7,5},{8,10},{9,11},{10,... | collective-permute-start | bytes 786440 | tf_op jit(solution)/shard_map/ppermute | solution.py:472
  27.3 13.4 %collective-permute-start.4 = (f32[512,128]{1,0:T(8,128)S(1)}, f32[512,128]{1,0:T(8,128)S(1)}, u32[]{:S(2)}, u32[]{:S(2)}) collective-permute-start(f32[512,128]{1,0:T(8,128)S(1)} %get-tuple-element.50), channel_id=1, source_target_pairs={{0,3},{1,2},{2,1},{3,0},{4,7},{5,6},{6,5},{7,4},{8,11},{9,10},{10,... | collective-permute-start | bytes 786440 | tf_op jit(solution)/shard_map/ppermute | solution.py:472
  28.2 24.1 %collective-permute-start.6 = (f32[512,128]{1,0:T(8,128)S(1)}, f32[512,128]{1,0:T(8,128)S(1)}, u32[]{:S(2)}, u32[]{:S(2)}) collective-permute-start(f32[512,128]{1,0:T(8,128)S(1)} %get-tuple-element.56), channel_id=1, source_target_pairs={{0,2},{1,3},{2,0},{3,1},{4,6},{5,7},{6,4},{7,5},{8,10},{9,11},{10,... | collective-permute-start | bytes 786440 | tf_op jit(solution)/shard_map/ppermute | solution.py:472
  29.4 22.8 %collective-permute-start.7 = (f32[512,128]{1,0:T(8,128)S(1)}, f32[512,128]{1,0:T(8,128)S(1)}, u32[]{:S(2)}, u32[]{:S(2)}) collective-permute-start(f32[512,128]{1,0:T(8,128)S(1)} %get-tuple-element.57), channel_id=1, source_target_pairs={{0,3},{1,2},{2,1},{3,0},{4,7},{5,6},{6,5},{7,4},{8,11},{9,10},{10,... | collective-permute-start | bytes 786440 | tf_op jit(solution)/shard_map/ppermute | solution.py:472
  41.5 15.6 %collective-permute-start.8 = (f32[1024,128]{1,0:T(8,128)S(1)}, f32[1024,128]{1,0:T(8,128)S(1)}, u32[]{:S(2)}, u32[]{:S(2)}) collective-permute-start(f32[1024,128]{1,0:T(8,128)S(1)} %halo_message.4), channel_id=1, source_target_pairs={{0,4},{1,5},{2,6},{3,7},{4,8},{5,9},{6,10},{7,11},{8,12},{9,13},{1... | collective-permute-start | bytes 1572872 | tf_op jit(solution)/shard_map/ppermute | solution.py:469
  53.1 15.4 %collective-permute-start.9 = (f32[1024,128]{1,0:T(8,128)S(1)}, f32[1024,128]{1,0:T(8,128)S(1)}, u32[]{:S(2)}, u32[]{:S(2)}) collective-permute-start(f32[1024,128]{1,0:T(8,128)S(1)} %halo_message.5), channel_id=1, source_target_pairs={{0,4},{1,5},{2,6},{3,7},{4,8},{5,9},{6,10},{7,11},{8,12},{9,13},{1... | collective-permute-start | bytes 1572872 | tf_op jit(solution)/shard_map/ppermute | solution.py:469
  54.5 24.2 %collective-permute-start.10 = (f32[960,128]{1,0:T(8,128)S(1)}, f32[960,128]{1,0:T(8,128)S(1)}, u32[]{:S(2)}, u32[]{:S(2)}) collective-permute-start(f32[960,128]{1,0:T(8,128)S(1)} %get-tuple-element.64), channel_id=1, source_target_pairs={{0,12},{1,13},{2,14},{3,15},{4,0},{5,1},{6,2},{7,3},{8,4},{9,5},{1... | collective-permute-start | bytes 1474568 | tf_op jit(solution)/shard_map/ppermute | solution.py:469
  66.5 24.4 %collective-permute-start.13 = (f32[960,128]{1,0:T(8,128)S(1)}, f32[960,128]{1,0:T(8,128)S(1)}, u32[]{:S(2)}, u32[]{:S(2)}) collective-permute-start(f32[960,128]{1,0:T(8,128)S(1)} %get-tuple-element.69), channel_id=1, source_target_pairs={{0,12},{1,13},{2,14},{3,15},{4,0},{5,1},{6,2},{7,3},{8,4},{9,5},{1... | collective-permute-start | bytes 1474568 | tf_op jit(solution)/shard_map/ppermute | solution.py:469
  77.9 24.9 %collective-permute-start.16 = (f32[960,128]{1,0:T(8,128)S(1)}, f32[960,128]{1,0:T(8,128)S(1)}, u32[]{:S(2)}, u32[]{:S(2)}) collective-permute-start(f32[960,128]{1,0:T(8,128)S(1)} %get-tuple-element.74), channel_id=1, source_target_pairs={{0,12},{1,13},{2,14},{3,15},{4,0},{5,1},{6,2},{7,3},{8,4},{9,5},{1... | collective-permute-start | bytes 1474568 | tf_op jit(solution)/shard_map/ppermute | solution.py:469
  79.7 5.9 %collective-permute-start.11 = (f32[384,128]{1,0:T(8,128)S(1)}, f32[384,128]{1,0:T(8,128)S(1)}, u32[]{:S(2)}, u32[]{:S(2)}) collective-permute-start(f32[384,128]{1,0:T(8,128)S(1)} %get-tuple-element.65), channel_id=1, source_target_pairs={{0,2},{1,3},{2,0},{3,1},{4,6},{5,7},{6,4},{7,5},{8,10},{9,11},{10,... | collective-permute-start | bytes 589832 | tf_op jit(solution)/shard_map/ppermute | solution.py:472
  81.2 9.7 %collective-permute-start.12 = (f32[384,128]{1,0:T(8,128)S(1)}, f32[384,128]{1,0:T(8,128)S(1)}, u32[]{:S(2)}, u32[]{:S(2)}) collective-permute-start(f32[384,128]{1,0:T(8,128)S(1)} %get-tuple-element.66), channel_id=1, source_target_pairs={{0,3},{1,2},{2,1},{3,0},{4,7},{5,6},{6,5},{7,4},{8,11},{9,10},{10,... | collective-permute-start | bytes 589832 | tf_op jit(solution)/shard_map/ppermute | solution.py:472
  91.8 6.7 %collective-permute-start.14 = (f32[384,128]{1,0:T(8,128)S(1)}, f32[384,128]{1,0:T(8,128)S(1)}, u32[]{:S(2)}, u32[]{:S(2)}) collective-permute-start(f32[384,128]{1,0:T(8,128)S(1)} %get-tuple-element.70), channel_id=1, source_target_pairs={{0,2},{1,3},{2,0},{3,1},{4,6},{5,7},{6,4},{7,5},{8,10},{9,11},{10,... | collective-permute-start | bytes 589832 | tf_op jit(solution)/shard_map/ppermute | solution.py:472
  93.4 9.4 %collective-permute-start.15 = (f32[384,128]{1,0:T(8,128)S(1)}, f32[384,128]{1,0:T(8,128)S(1)}, u32[]{:S(2)}, u32[]{:S(2)}) collective-permute-start(f32[384,128]{1,0:T(8,128)S(1)} %get-tuple-element.71), channel_id=1, source_target_pairs={{0,3},{1,2},{2,1},{3,0},{4,7},{5,6},{6,5},{7,4},{8,11},{9,10},{10,... | collective-permute-start | bytes 589832 | tf_op jit(solution)/shard_map/ppermute | solution.py:472
  103.8 11.3 %collective-permute-start.17 = (f32[1152,128]{1,0:T(8,128)S(1)}, f32[1152,128]{1,0:T(8,128)S(1)}, u32[]{:S(2)}, u32[]{:S(2)}) collective-permute-start(f32[1152,128]{1,0:T(8,128)S(1)} %get-tuple-element.77), channel_id=1, source_target_pairs={{0,1},{1,0},{2,3},{3,2},{4,5},{5,4},{6,7},{7,6},{8,9},{9,8},{10,11... | collective-permute-start | bytes 1769480 | tf_op jit(solution)/shard_map/ppermute | solution.py:472
  104.2 6.5 %collective-permute-start.18 = (f32[384,128]{1,0:T(8,128)S(1)}, f32[384,128]{1,0:T(8,128)S(1)}, u32[]{:S(2)}, u32[]{:S(2)}) collective-permute-start(f32[384,128]{1,0:T(8,128)S(1)} %get-tuple-element.81), channel_id=1, source_target_pairs={{0,2},{1,3},{2,0},{3,1},{4,6},{5,7},{6,4},{7,5},{8,10},{9,11},{10,... | collective-permute-start | bytes 589832 | tf_op jit(solution)/shard_map/ppermute | solution.py:472
  105.5 9.6 %collective-permute-start.19 = (f32[384,128]{1,0:T(8,128)S(1)}, f32[384,128]{1,0:T(8,128)S(1)}, u32[]{:S(2)}, u32[]{:S(2)}) collective-permute-start(f32[384,128]{1,0:T(8,128)S(1)} %get-tuple-element.82), channel_id=1, source_target_pairs={{0,3},{1,2},{2,1},{3,0},{4,7},{5,6},{6,5},{7,4},{8,11},{9,10},{10,... | collective-permute-start | bytes 589832 | tf_op jit(solution)/shard_map/ppermute | solution.py:472
